TPU v7x, 128 devices: a whole 4x4x4 slice. The times are simulated.
128 devices in a mesh: rows: 32 (over x_hi, z, y), layers: 4 (over x_lo, core).
Axes of the slice: x: 4 (x_hi: 2, x_lo: 2; x = x_hi * 2 + x_lo), y: 4, z: 4, core: 2. Of those that a mesh axis runs over, the one named last changes fastest.
Arguments:
- queries: bfloat16 [1024, 4, 4096], P('rows', 'layers'), may hold values from -6 to 6
- precond: bfloat16 [4, 4096, 4096], P('layers', None, 'rows'), as said below
- train_grads: bfloat16 [65536, 4, 4096], P('rows', 'layers'), may hold values from -0.09375 to 0.09375
Outputs:
- scores: float32 [1024, 65536], P('layers', 'rows')
Inputs may be any that keep to these rules, and one draw needn't show every extreme that they name: `precond`: symmetric in its last two dimensions.
All inputs are finite; a program needn't handle non-finite values.
Results may differ from a plain program's by a relative error of at most 0.0029.
Values may be sent and summed in bfloat16 or wider, within the bound.
No kernel may reach another device: no remote copies, remote signals or barrier semaphores. Data moves between devices by JAX's collectives and lax.ppermute only.
A program may use at most 128 MiB of HBM per device.

v0:
```python
import jax
import jax.numpy as jnp
from jax import lax
from jax.sharding import PartitionSpec as P


def per_device(queries, precond, train_grads):
    all_queries = lax.all_gather(queries, "rows", axis=0, tiled=True)
    cond_cols = jnp.einsum(
        "qlf,lfc->qlc", all_queries, precond, preferred_element_type=jnp.float32
    ).astype(jnp.bfloat16)
    partial_scores = jnp.einsum(
        "qlc,tlc->qt",
        lax.all_gather(cond_cols, "rows", axis=2, tiled=True),
        train_grads,
        preferred_element_type=jnp.float32,
    )
    return lax.psum_scatter(partial_scores, "layers", scatter_dimension=0, tiled=True)


def solution(mesh):
    return jax.shard_map(
        per_device,
        mesh=mesh,
        in_specs=(P("rows", "layers", None), P("layers", None, "rows"), P("rows", "layers", None)),
        out_specs=P("layers", "rows"),
        check_vma=False,
    )
```

profile of v0, /device:TPU:1, one launch (start us, length us, event | category | flops | bytes accessed | tf_op | source)
XLA Modules:
  0.0 334.6 jit_solution(17935776267385297126)
XLA Ops:
  6.5 0.0 copy-start
  6.5 0.0 all-gather.3.cloned.1.call-start
  6.5 0.7 all-gather.3.cloned.1.call-update
  7.3 0.0 all-gather.5.cloned.1.call-start
  7.3 109.8 %all-gather.3.cloned.1.call-done = bf16[1024,1,4096]{2,0,1:T(8,128)(2,1)} async-done(((bf16[32,1,4096]{2,0,1:T(8,128)(2,1)}), bf16[1024,1,4096]{2,0,1:T(8,128)(2,1)}) %all-gather.3.cloned.1.call-update) | async-done | bytes 8388624 | tf_op jit(solution)/shard_map/all_gather | solution.py:8
  117.1 0.0 copy-done
  117.1 7.0 %fusion.8 = bf16[1024,1,128]{0,2,1:T(8,128)(2,1)} fusion(bf16[1024,1,4096]{2,0,1:T(8,128)(2,1)} %all-gather.3.cloned.1.call-done, bf16[1,4096,128]{2,1,0:T(8,128)(2,1)S(1)} %copy-done), kind=kOutput, calls=%fused_computation.6 | convolution fusion | flops 1073872896 | bytes 9699328 | tf_op jit(solution)/shard_map/qlf,lfc->qlc/dot_general | solution.py:9
  124.1 0.0 all-gather.5.cloned.1.call-update
  124.1 0.0 reduce-scatter.2.cloned.1.call-start
  124.2 101.9 %all-gather.5.cloned.1.call-done = bf16[1024,1,4096]{0,2,1:T(8,128)(2,1)} async-done(((bf16[1024,1,128]{0,2,1:T(8,128)(2,1)}), bf16[1024,1,4096]{0,2,1:T(8,128)(2,1)}) %all-gather.5.cloned.1.call-update) | async-done | bytes 8388624 | tf_op jit(solution)/shard_map/all_gather | solution.py:14
  226.1 24.2 %fusion = f32[1024,2048]{1,0:T(8,128)} fusion(bf16[2048,1,4096]{2,0,1:T(8,128)(2,1)} %param.5, bf16[1024,1,4096]{0,2,1:T(8,128)(2,1)} %all-gather.5.cloned.1.call-done), kind=kOutput, calls=%fused_computation | convolution fusion | flops 17179869184 | bytes 33554432 | tf_op jit(solution)/shard_map/qlc,tlc->qt/dot_general | solution.py:12
  250.2 0.0 reduce-scatter.2.cloned.1.call-update
  250.3 77.8 %reduce-scatter.2.cloned.1.call-done = f32[256,2048]{1,0:T(8,128)} async-done(((f32[1024,2048]{1,0:T(8,128)}), f32[256,2048]{1,0:T(8,128)}) %reduce-scatter.2.cloned.1.call-update) | async-done | bytes 2097168 | tf_op jit(solution)/shard_map/reduce_scatter | solution.py:18
Async XLA Ops:
  6.5 110.6 %copy-start = (bf16[1,4096,128]{2,1,0:T(8,128)(2,1)S(1)}, bf16[1,4096,128]{2,1,0:T(8,128)(2,1)}, u32[]{:S(2)}) copy-start(bf16[1,4096,128]{2,1,0:T(8,128)(2,1)} %param.4) | copy-start | bytes 3145732
  6.5 110.6 %all-gather.3.cloned.1.call-start = ((), (), s32[]{:S(2)}) async-start(), calls=%async_computation.1 | async-start | bytes 8650752 | tf_op jit(solution)/shard_map/all_gather | solution.py:8
  7.3 218.8 %all-gather.5.cloned.1.call-start = ((), (), s32[]{:S(2)}) async-start(), calls=%async_computation.2 | async-start | bytes 8650752 | tf_op jit(solution)/shard_map/all_gather | solution.py:14
  124.1 203.9 %reduce-scatter.2.cloned.1.call-start = ((), (), s32[]{:S(2)}) async-start(), calls=%async_computation.3 | async-start | bytes 10485760 | tf_op jit(solution)/shard_map/reduce_scatter | solution.py:18
Sparse Core Ops, SparseCore 0:
  10.4 106.6 all-gather.2
  124.2 101.7 all-gather.4
  250.4 77.6 reduce-scatter.1
where the time goes:
time: 335 us
  waiting for transfers between devices  290 us (87%)
  matrix products  31.2 us (9%)
  between operations  13.1 us (4%)
    all_gather x1, waiting for transfers between devices, per_device(): all_queries = lax.all_gather(queries, 'rows', axis=0, tiled=True)  110 us
    all_gather x1, waiting for transfers between devices, per_device(): lax.all_gather(cond_cols, 'rows', axis=2, tiled=True)  102 us
    reduce_scatter x1, waiting for transfers between devices, per_device(): lax.psum_scatter(partial_scores, 'layers', scatter_dimension=0, tiled=True)  77.8 us
    dot_general x1, matrix products, per_device(): jnp.einsum('qlc,tlc->qt', lax.all_gather(cond_cols, 'rows', axis=2, tiled...  24.2 us
    dot_general x1, matrix products, per_device(): jnp.einsum('qlf,lfc->qlc', all_queries, precond, preferred_element_type=j...  6.99 us
  transfers between devices with their start and end apart: 3, of which 3 were waited for; matrix products, arithmetic and copies ran while one was open for 0% of the time, Pallas kernels for 0%

commit v1 on v0

v1 whole, which is shorter than its diff:
```python
import functools

import jax
import jax.numpy as jnp
from jax import lax
from jax.experimental import pallas as pl
from jax.experimental.pallas import tpu as pltpu
from jax.sharding import PartitionSpec as P

F = 4096
COLS = 128
SUB = 16
RA = 16 * SUB
TT = 512
NTL = 2048
TILES = (((0, 4),), ((0, 3), (3, 1)))


def perm_of(f):
    pairs = []
    for r in range(32):
        xh, z, y = r // 16, (r // 4) % 4, r % 4
        a, b, c = f(xh, z, y)
        pairs.append((r, (a % 2) * 16 + (b % 4) * 4 + c % 4))
    return pairs


UP_Y = perm_of(lambda a, b, c: (a, b, c + 1))
DOWN_Y = perm_of(lambda a, b, c: (a, b, c - 1))
UP_Z = perm_of(lambda a, b, c: (a, b + 1, c))
DOWN_Z = perm_of(lambda a, b, c: (a, b - 1, c))
CORNER = perm_of(lambda a, b, c: (a, b + 2, c + 2))
XH = perm_of(lambda a, b, c: (a + 1, b, c))
CORE = [(0, 1), (1, 0), (2, 3), (3, 2)]
XL = [(0, 2), (2, 0), (1, 3), (3, 1)]


def send4(to_up_y, to_down_y, to_up_z, to_down_z):
    return [
        lax.ppermute(x, "rows", perm)
        for x, perm in ((to_up_y, UP_Y), (to_down_y, DOWN_Y), (to_up_z, UP_Z), (to_down_z, DOWN_Z))
    ]


NEAR = ((0, 0), (0, 3), (0, 1), (3, 0), (1, 0))
DIAGONAL = ((3, 3), (1, 1), (3, 1), (1, 3))
FAR = ((0, 2), (0, 2), (2, 0), (2, 0))
KNIGHT = ((3, 2), (1, 2), (2, 1), (2, 3))


def flood(block):
    near = [block] + send4(block, block, block, block)
    _, ly, ry, lz, rz = near
    cat = lambda a, b: jnp.concatenate([a, b], axis=0)
    two = send4(cat(lz, ly[:1]), cat(rz, ry[1:]), cat(ry, lz[:1]), cat(ly, rz[1:]))
    three = send4(*[x[:2] for x in two])
    return [*near, *two, *three, lax.ppermute(block, "rows", CORNER)]


def condition_kernel(pos, *refs):
    near, two, three, (corner, own, other, out, q, p, sem) = refs[:5], refs[5:9], refs[9:13], refs[13:]
    xh, z, y = pos[0], pos[1], pos[2]
    at = lambda d: ((z + d[0]) % 4) * 4 + (y + d[1]) % 4
    copies = [(own, p.at[:, pl.ds(pl.multiple_of(xh * COLS, COLS), COLS)])]
    copies += [(other, p.at[:, pl.ds(pl.multiple_of((1 - xh) * COLS, COLS), COLS)])]
    copies += [(x, q.at[at(d)]) for x, d in zip(near, NEAR)]
    copies += [(x.at[0:2], q.at[at(d)]) for x, d in zip(two, DIAGONAL)]
    copies += [(x.at[2], q.at[at(d), k % 2]) for k, (x, d) in enumerate(zip(two, FAR))]
    copies += [(x, q.at[at(d)]) for x, d in zip(three, KNIGHT)]
    copies += [(corner, q.at[at((2, 2))])]
    copies = [pltpu.make_async_copy(src, dst, sem.at[i]) for i, (src, dst) in enumerate(copies)]
    for c in copies:
        c.start()
    for c in copies:
        c.wait()
    s = jnp.dot(q[...].reshape(2 * RA, F), p[...], preferred_element_type=jnp.float32)
    s = s.astype(jnp.bfloat16).reshape(16, 2, SUB, 2 * COLS)
    for chunk in range(2):
        for h in range(2):
            out[chunk, h] = s[:, chunk, :, h * COLS : (h + 1) * COLS].reshape(RA, COLS)


def condition(pos, pieces, own, other):
    return pl.pallas_call(
        condition_kernel,
        out_shape=jax.ShapeDtypeStruct((2, 2, RA, COLS), jnp.bfloat16),
        in_specs=[pl.BlockSpec(memory_space=pltpu.SMEM)] + [pl.BlockSpec(memory_space=pltpu.HBM)] * 16,
        out_specs=pl.BlockSpec(memory_space=pltpu.VMEM),
        scratch_shapes=[
            pltpu.VMEM((16, 2, SUB, F), jnp.bfloat16),
            pltpu.VMEM((F, 2 * COLS), jnp.bfloat16),
            pltpu.SemaphoreType.DMA((20,)),
        ],
        compiler_params=pltpu.CompilerParams(vmem_limit_bytes=24 << 20),
        cost_estimate=pl.CostEstimate(flops=4 * RA * F * 256, bytes_accessed=6 << 20, transcendentals=0),
        name="condition",
    )(pos, *pieces, own, other)


def score_kernel(chunk, pos, *refs):
    near, two, three, (corner, t, keep, send, c, sem) = refs[:5], refs[5:9], refs[9:13], refs[13:]
    xh, z, y, xl, core = (pos[i] for i in range(5))

    @pl.when(pl.program_id(0) == 0)
    def _():
        at = lambda d: c.at[:, :, :, pl.ds(pl.multiple_of((((z + d[0]) % 4) * 4 + (y + d[1]) % 4) * COLS, COLS), COLS)]
        copies = [(x.at[chunk], at(d)) for x, d in zip(near, NEAR)]
        copies += [(x.at[chunk], at(d)) for x, d in zip(two, DIAGONAL)]
        copies += [(two[k].at[2], at(FAR[k])) for k in (chunk, 2 + chunk)]
        copies += [(x.at[chunk], at(d)) for x, d in zip(three, KNIGHT)]
        copies += [(corner.at[chunk], at((2, 2)))]
        copies = [pltpu.make_async_copy(src, dst, sem.at[i]) for i, (src, dst) in enumerate(copies)]
        for x in copies:
            x.start()
        for x in copies:
            x.wait()

    s = 0.0
    for h in range(2):
        s += lax.dot_general(
            c[:, h].reshape(2 * RA, F // 2),
            t[:, h * (F // 2) : (h + 1) * (F // 2)],
            (((1,), (1,)), ((), ())),
            preferred_element_type=jnp.float32,
        )
    s = s.reshape(2, 2, RA // 2, TT)
    same = xh == xl
    for i in range(2):
        own = jnp.where(same, s[i], s[1 - i])
        keep[i] = jnp.where(core == 0, own[0], own[1])
        send[i] = jnp.where(core == 0, own[1], own[0]).astype(jnp.bfloat16)


def score(pos, pieces, train, chunk, first, steps):
    return pl.pallas_call(
        functools.partial(score_kernel, chunk),
        grid=(steps,),
        out_shape=(
            jax.ShapeDtypeStruct((2, RA // 2, steps * TT), jnp.float32),
            jax.ShapeDtypeStruct((2, RA // 2, steps * TT), jnp.bfloat16),
        ),
        in_specs=[pl.BlockSpec(memory_space=pltpu.SMEM)]
        + [pl.BlockSpec(memory_space=pltpu.HBM)] * 14
        + [pl.BlockSpec((TT, F), lambda i: (i + first, 0))],
        out_specs=(
            pl.BlockSpec((2, RA // 2, TT), lambda i: (0, 0, i)),
            pl.BlockSpec((2, RA // 2, TT), lambda i: (0, 0, i)),
        ),
        scratch_shapes=[pltpu.VMEM((2, 2, RA, F // 2), jnp.bfloat16), pltpu.SemaphoreType.DMA((16,))],
        compiler_params=pltpu.CompilerParams(vmem_limit_bytes=36 << 20),
        cost_estimate=pl.CostEstimate(
            flops=2 * 2 * RA * F * steps * TT, bytes_accessed=(RA * F * 4 + steps * TT * F * 2), transcendentals=0
        ),
        name="score",
    )(pos, *pieces, train)


def per_device(queries, precond, train_grads):
    r, l = lax.axis_index("rows"), lax.axis_index("layers")
    pos = jnp.stack([r // 16, (r // 4) % 4, r % 4, l // 2, l % 2]).astype(jnp.int32)
    q = queries.reshape(2, SUB, F)
    p = precond.reshape(F, COLS)
    train = pltpu.with_memory_space_constraint(train_grads.reshape(NTL, F), pltpu.HBM)
    p_other = lax.ppermute(p, "rows", XH)

    cond = condition(pos, flood(q), p, p_other)

    partner = lax.ppermute(cond, "rows", XH)
    pieces = flood(jnp.stack([cond, partner], axis=1))
    out = jnp.zeros((8, 2, SUB, NTL), jnp.float32)
    for chunk in range(2):
        for first, steps in TILES[chunk]:
            keep, send = score(pos, pieces, train, chunk, first, steps)
            got = lax.ppermute(send, "layers", CORE)
            away = (keep[1] + got[1].astype(jnp.float32)).astype(jnp.bfloat16)
            if chunk == 0:
                pos, away = lax.optimization_barrier((pos, away))
            back = lax.ppermute(away, "layers", XL)
            total = keep[0] + got[0].astype(jnp.float32) + back.astype(jnp.float32)
            out = lax.dynamic_update_slice(out, total.reshape(8, 1, SUB, steps * TT), (0, chunk, 0, first * TT))
            if chunk == 0:
                pos_late, out = lax.optimization_barrier((pos, out))
            elif first == 0:
                pos = pos_late
    return out.reshape(256, NTL)


def solution(mesh):
    return jax.shard_map(
        per_device,
        mesh=mesh,
        in_specs=(P("rows", "layers", None), P("layers", None, "rows"), P("rows", "layers", None)),
        out_specs=P("layers", "rows"),
        check_vma=False,
    )
```

time: 335 us -> 173 us (0.52)
  waiting for transfers between devices: 290 us -> 72 us
  starting transfers between devices: 0.08 us -> 57.7 us
  Pallas kernels: 0 us -> 35 us
  matrix products: 31.2 us -> 0 us
  between operations: 13.1 us -> 0.31 us
  local copies, waits for them, and re-layouts: 0.01 us -> 6.28 us
    all_gather x2 -> x0, waiting for transfers between devices: 212 us -> none  [the longest x1 110 us: per_device(): all_queries = lax.all_gather(queries, 'rows', axis=0, tiled=True)]
    reduce_scatter x1 -> x0, waiting for transfers between devices: 77.8 us -> none  [per_device(): lax.psum_scatter(partial_scores, 'layers', scatter_dimension=0, tiled=True)]
    ppermute x0 -> x34, waiting for transfers between devices: none -> 72 us  [the longest x24 51.8 us: send4(): lax.ppermute(x, 'rows', perm)]
    ppermute x0 -> x34, starting transfers between devices: none -> 57.7 us  [the longest x24 27.5 us: send4(): lax.ppermute(x, 'rows', perm)]
    pallas_call x0 -> x4, Pallas kernels: none -> 35 us  [the longest x3 30.8 us: score(): pl.pallas_call(functools.partial(score_kernel, chunk), grid=(steps,), out...]
    dot_general x2 -> x0, matrix products: 31.2 us -> none  [the longest x1 24.2 us: per_device(): jnp.einsum('qlc,tlc->qt', lax.all_gather(cond_cols, 'rows', axis=2, tiled...]
  transfers between devices with their start and end apart: 3 -> 34, of which waited for: 3 -> 22; matrix products, arithmetic and copies ran while one was open for 0% -> 2% of each run, Pallas kernels for 0% -> 10%
where the time goes in v1:
time: 173 us; the launch traced here: 172 us
  waiting for transfers between devices  72 us (42%)
  starting transfers between devices  57.7 us (33%)
  Pallas kernels  35 us (20%)
  local copies, waits for them, and re-layouts  6.28 us (4%)
    ppermute x24, waiting for transfers between devices, send4(): lax.ppermute(x, 'rows', perm)  51.8 us
    pallas_call x3, Pallas kernels, score(): pl.pallas_call(functools.partial(score_kernel, chunk), grid=(steps,), out...  30.8 us
    ppermute x24, starting transfers between devices, send4(): lax.ppermute(x, 'rows', perm)  27.5 us
    ppermute x3, starting transfers between devices, per_device(): got = lax.ppermute(send, 'layers', CORE)  14.9 us
    ppermute x3, waiting for transfers between devices, per_device(): back = lax.ppermute(away, 'layers', XL)  11.7 us
    ppermute x2, starting transfers between devices, flood(): return [*near, *two, *three, lax.ppermute(block, 'rows', CORNER)]  6.68 us
    pallas_call x1, Pallas kernels, condition(): pl.pallas_call(condition_kernel, out_shape=jax.ShapeDtypeStruct((2, 2, RA...  4.28 us
    ppermute x1, waiting for transfers between devices, per_device(): partner = lax.ppermute(cond, 'rows', XH)  4.09 us
  transfers between devices with their start and end apart: 34, of which 22 were waited for; matrix products, arithmetic and copies ran while one was open for 2% of the time, Pallas kernels for 10%

profile of v1, /device:TPU:1, one launch (start us, length us, event | category | flops | bytes accessed | tf_op | source)
XLA Modules:
  0.0 172.3 jit_solution(5133023724853655230)
XLA Ops:
  0.0 2.5 %collective-permute-start.2 = (bf16[2,16,4096]{2,1,0:T(8,128)(2,1)}, bf16[2,16,4096]{2,1,0:T(8,128)(2,1)S(1)}, u32[]{:S(2)}, u32[]{:S(2)}) collective-permute-start(bf16[2,16,4096]{2,1,0:T(8,128)(2,1)} %bitcast.29), channel_id=1, source_target_pairs={{0,16},{4,20},{8,24},{12,28},{16,32},{20,36},{24,40},{28,44},{32,4... | collective-permute-start | bytes 786440 | tf_op jit(solution)/shard_map/ppermute | solution.py:40
  2.5 2.7 %collective-permute-start.1 = (bf16[2,16,4096]{2,1,0:T(8,128)(2,1)}, bf16[2,16,4096]{2,1,0:T(8,128)(2,1)S(1)}, u32[]{:S(2)}, u32[]{:S(2)}) collective-permute-start(bf16[2,16,4096]{2,1,0:T(8,128)(2,1)} %bitcast.30), channel_id=1, source_target_pairs={{0,12},{4,0},{8,4},{12,8},{16,28},{20,16},{24,20},{28,24},{32,44},... | collective-permute-start | bytes 786440 | tf_op jit(solution)/shard_map/ppermute | solution.py:40
  7.3 2.7 %collective-permute-start.13 = (bf16[4096,128]{1,0:T(8,128)(2,1)}, bf16[4096,128]{1,0:T(8,128)(2,1)}, u32[]{:S(2)}, u32[]{:S(2)}) collective-permute-start(bf16[4096,128]{1,0:T(8,128)(2,1)} %bitcast.26), channel_id=1, source_target_pairs={{0,64},{4,68},{8,72},{12,76},{16,80},{20,84},{24,88},{28,92},{32,9... | collective-permute-start | bytes 3145736 | tf_op jit(solution)/shard_map/ppermute | solution.py:164
  12.4 3.0 %collective-permute-done.refs_1_ = bf16[2,16,4096]{2,1,0:T(8,128)(2,1)S(1)} collective-permute-done((bf16[2,16,4096]{2,1,0:T(8,128)(2,1)}, bf16[2,16,4096]{2,1,0:T(8,128)(2,1)S(1)}, u32[]{:S(2)}, u32[]{:S(2)}) %collective-permute-start) | collective-permute-done | bytes 262176 | tf_op jit(solution)/shard_map/ppermute | solution.py:40
  16.9 2.7 %collective-permute-start.5 = (bf16[3,16,4096]{2,1,0:T(8,128)(2,1)S(1)}, bf16[3,16,4096]{2,1,0:T(8,128)(2,1)S(1)}, u32[]{:S(2)}, u32[]{:S(2)}) collective-permute-start(bf16[3,16,4096]{2,1,0:T(8,128)(2,1)S(1)} %pad_maximum_fusion.6), channel_id=1, source_target_pairs={{0,12},{4,0},{8,4},{12,8},{16,28},{20,16},{24,20},{28,24},{32,44},... | collective-permute-start | bytes 1179656 | tf_op jit(solution)/shard_map/ppermute | solution.py:40
  21.7 2.8 %collective-permute-start.12 = (bf16[2,16,4096]{2,1,0:T(8,128)(2,1)S(1)}, bf16[2,16,4096]{2,1,0:T(8,128)(2,1)S(1)}, u32[]{:S(2)}, u32[]{:S(2)}) collective-permute-start(bf16[2,16,4096]{2,1,0:T(8,128)(2,1)S(1)} %bitcast.33), channel_id=1, source_target_pairs={{0,40},{4,44},{8,32},{12,36},{16,56},{20,60},{24,48},{28,52},{32,8... | collective-permute-start | bytes 786440 | tf_op jit(solution)/shard_map/ppermute | solution.py:57
  33.3 6.2 %collective-permute-done.10.refs_11_ = bf16[2,16,4096]{2,1,0:T(8,128)(2,1)S(1)} collective-permute-done((bf16[2,16,4096]{2,1,0:T(8,128)(2,1)}, bf16[2,16,4096]{2,1,0:T(8,128)(2,1)S(1)}, u32[]{:S(2)}, u32[]{:S(2)}) %collective-permute-start.10) | collective-permute-done | bytes 262176 | tf_op jit(solution)/shard_map/ppermute | solution.py:40
  40.7 4.3 %condition.1 = bf16[2,2,256,128]{3,2,1,0:T(8,128)(2,1)S(1)} custom-call(s32[5]{0:T(128)S(1)} %stack.32.pos, bf16[2,16,4096]{2,1,0:T(8,128)(2,1)S(1)} %bitcast.34, bf16[2,16,4096]{2,1,0:T(8,128)(2,1)S(1)} %collective-permute-done.refs_1_, bf16[2,16,4096]{2,1,0:T(8,128)(2,1)S(1)} %collective-permute-done.1.refs_2_, ...), custom_call_target="tpu_custom_call" | custom-call | flops 1073741824 | bytes 6291456 | tf_op jit(solution)/shard_map/condition/pallas_call | solution.py:84
  45.0 2.7 %collective-permute-start.14 = (bf16[2,2,256,128]{3,2,1,0:T(8,128)(2,1)S(1)}, bf16[2,2,256,128]{3,2,1,0:T(8,128)(2,1)S(1)}, u32[]{:S(2)}, u32[]{:S(2)}) collective-permute-start(bf16[2,2,256,128]{3,2,1,0:T(8,128)(2,1)S(1)} %condition.1), channel_id=1, source_target_pairs={{0,64},{4,68},{8,72},{12,76},{16,80},{20,84},{24,88},{28,92},{32,9... | collective-permute-start | bytes 786440 | tf_op jit(solution)/shard_map/ppermute | solution.py:168
  47.7 4.1 %collective-permute-done.14 = bf16[2,2,256,128]{3,2,1,0:T(8,128)(2,1)S(1)} collective-permute-done((bf16[2,2,256,128]{3,2,1,0:T(8,128)(2,1)S(1)}, bf16[2,2,256,128]{3,2,1,0:T(8,128)(2,1)S(1)}, u32[]{:S(2)}, u32[]{:S(2)}) %collective-permute-start.14) | collective-permute-done | bytes 262176 | tf_op jit(solution)/shard_map/ppermute | solution.py:168
  56.2 3.7 %collective-permute-done.18.refs_4_ = bf16[2,2,2,256,128]{4,3,2,1,0:T(8,128)(2,1)S(1)} collective-permute-done((bf16[2,2,2,256,128]{4,3,2,1,0:T(8,128)(2,1)S(1)}, bf16[2,2,2,256,128]{4,3,2,1,0:T(8,128)(2,1)S(1)}, u32[]{:S(2)}, u32[]{:S(2)}) %collective-permute-start.18) | collective-permute-done | bytes 524320 | tf_op jit(solution)/shard_map/ppermute | solution.py:40
  60.0 2.8 %collective-permute-done.15.refs_1_ = bf16[2,2,2,256,128]{4,3,2,1,0:T(8,128)(2,1)S(1)} collective-permute-done((bf16[2,2,2,256,128]{4,3,2,1,0:T(8,128)(2,1)S(1)}, bf16[2,2,2,256,128]{4,3,2,1,0:T(8,128)(2,1)S(1)}, u32[]{:S(2)}, u32[]{:S(2)}) %collective-permute-start.15) | collective-permute-done | bytes 524320 | tf_op jit(solution)/shard_map/ppermute | solution.py:40
  67.4 3.9 %collective-permute-start.27 = (bf16[2,2,2,256,128]{4,3,2,1,0:T(8,128)(2,1)S(1)}, bf16[2,2,2,256,128]{4,3,2,1,0:T(8,128)(2,1)S(1)}, u32[]{:S(2)}, u32[]{:S(2)}) collective-permute-start(bf16[2,2,2,256,128]{4,3,2,1,0:T(8,128)(2,1)S(1)} %pad_maximum_fusion.4.refs_0_), channel_id=1, source_target_pairs={{0,40},{4,44},{8,32},{12,36},{16,56},{20,60},{24,48},{28,52},{32,8... | collective-permute-start | bytes 1572872 | tf_op jit(solution)/shard_map/ppermute | solution.py:57
  71.3 5.6 %collective-permute-done.22.refs_8_ = bf16[3,2,2,256,128]{4,3,2,1,0:T(8,128)(2,1)S(1)} collective-permute-done((bf16[3,2,2,256,128]{4,3,2,1,0:T(8,128)(2,1)S(1)}, bf16[3,2,2,256,128]{4,3,2,1,0:T(8,128)(2,1)S(1)}, u32[]{:S(2)}, u32[]{:S(2)}) %collective-permute-start.22) | collective-permute-done | bytes 786464 | tf_op jit(solution)/shard_map/ppermute | solution.py:40
  79.0 7.2 %collective-permute-done.20.refs_6_ = bf16[3,2,2,256,128]{4,3,2,1,0:T(8,128)(2,1)S(1)} collective-permute-done((bf16[3,2,2,256,128]{4,3,2,1,0:T(8,128)(2,1)S(1)}, bf16[3,2,2,256,128]{4,3,2,1,0:T(8,128)(2,1)S(1)}, u32[]{:S(2)}, u32[]{:S(2)}) %collective-permute-start.20) | collective-permute-done | bytes 786464 | tf_op jit(solution)/shard_map/ppermute | solution.py:40
  86.2 3.5 %collective-permute-start.24 = (bf16[2,2,2,256,128]{4,3,2,1,0:T(8,128)(2,1)S(1)}, bf16[2,2,2,256,128]{4,3,2,1,0:T(8,128)(2,1)S(1)}, u32[]{:S(2)}, u32[]{:S(2)}) collective-permute-start(bf16[2,2,2,256,128]{4,3,2,1,0:T(8,128)(2,1)S(1)} %slice.125), channel_id=1, source_target_pairs={{0,12},{4,0},{8,4},{12,8},{16,28},{20,16},{24,20},{28,24},{32,44},... | collective-permute-start | bytes 1572872 | tf_op jit(solution)/shard_map/ppermute | solution.py:40
  90.4 5.4 %collective-permute-done.26.refs_12_ = bf16[2,2,2,256,128]{4,3,2,1,0:T(8,128)(2,1)S(1)} collective-permute-done((bf16[2,2,2,256,128]{4,3,2,1,0:T(8,128)(2,1)S(1)}, bf16[2,2,2,256,128]{4,3,2,1,0:T(8,128)(2,1)S(1)}, u32[]{:S(2)}, u32[]{:S(2)}) %collective-permute-start.26) | collective-permute-done | bytes 524320 | tf_op jit(solution)/shard_map/ppermute | solution.py:40
  95.8 4.0 %collective-permute-done.25.refs_11_ = bf16[2,2,2,256,128]{4,3,2,1,0:T(8,128)(2,1)S(1)} collective-permute-done((bf16[2,2,2,256,128]{4,3,2,1,0:T(8,128)(2,1)S(1)}, bf16[2,2,2,256,128]{4,3,2,1,0:T(8,128)(2,1)S(1)}, u32[]{:S(2)}, u32[]{:S(2)}) %collective-permute-start.25) | collective-permute-done | bytes 524320 | tf_op jit(solution)/shard_map/ppermute | solution.py:40
  99.8 5.0 %collective-permute-done.24.refs_10_ = bf16[2,2,2,256,128]{4,3,2,1,0:T(8,128)(2,1)S(1)} collective-permute-done((bf16[2,2,2,256,128]{4,3,2,1,0:T(8,128)(2,1)S(1)}, bf16[2,2,2,256,128]{4,3,2,1,0:T(8,128)(2,1)S(1)}, u32[]{:S(2)}, u32[]{:S(2)}) %collective-permute-start.24) | collective-permute-done | bytes 524320 | tf_op jit(solution)/shard_map/ppermute | solution.py:40
  107.0 13.6 %score.3 = (f32[2,128,2048]{2,1,0:T(8,128)S(1)}, bf16[2,128,2048]{2,1,0:T(8,128)(2,1)S(1)}) custom-call(s32[5]{0:T(128)S(1)} %stack.32.pos, bf16[2,2,2,256,128]{4,3,2,1,0:T(8,128)(2,1)S(1)} %pad_maximum_fusion.4.refs_0_, bf16[2,2,2,256,128]{4,3,2,1,0:T(8,128)(2,1)S(1)} %collective-permute-done.15.refs_1_, ...), custom_call_target="tpu_custom_call" | custom-call | flops 8589934592 | bytes 20971520 | tf_op jit(solution)/shard_map/score/pallas_call | solution.py:135
  120.6 12.9 %collective-permute-start.28 = (bf16[2,128,2048]{2,1,0:T(8,128)(2,1)S(1)}, bf16[2,128,2048]{2,1,0:T(8,128)(2,1)S(1)}, u32[]{:S(2)}, u32[]{:S(2)}) collective-permute-start(bf16[2,128,2048]{2,1,0:T(8,128)(2,1)S(1)} %get-tuple-element.16), channel_id=1, source_target_pairs={{0,1},{1,0},{2,3},{3,2},{4,5},{5,4},{6,7},{7,6},{8,9},{9,8},{10,11... | collective-permute-start | bytes 3145736 | tf_op jit(solution)/shard_map/ppermute | solution.py:174
  137.0 11.1 %score.4 = (f32[2,128,1536]{2,1,0:T(8,128)S(1)}, bf16[2,128,1536]{2,1,0:T(8,128)(2,1)S(1)}) custom-call(s32[5]{0:T(128)S(1)} %stack.32.pos, bf16[2,2,2,256,128]{4,3,2,1,0:T(8,128)(2,1)S(1)} %pad_maximum_fusion.4.refs_0_, bf16[2,2,2,256,128]{4,3,2,1,0:T(8,128)(2,1)S(1)} %collective-permute-done.15.refs_1_, ...), custom_call_target="tpu_custom_call" | custom-call | flops 6442450944 | bytes 16777216 | tf_op jit(solution)/shard_map/score/pallas_call | solution.py:135
  149.5 6.1 %score.5 = (f32[2,128,512]{2,1,0:T(8,128)S(1)}, bf16[2,128,512]{2,1,0:T(8,128)(2,1)S(1)}) custom-call(s32[5]{0:T(128)S(1)} %stack.32.pos, bf16[2,2,2,256,128]{4,3,2,1,0:T(8,128)(2,1)S(1)} %pad_maximum_fusion.4.refs_0_, bf16[2,2,2,256,128]{4,3,2,1,0:T(8,128)(2,1)S(1)} %collective-permute-done.15.refs_1_, ...), custom_call_target="tpu_custom_call" | custom-call | flops 2147483648 | bytes 8388608 | tf_op jit(solution)/shard_map/score/pallas_call | solution.py:135
  159.1 11.4 %collective-permute-done.33 = bf16[128,512]{1,0:T(8,128)(2,1)S(1)} collective-permute-done((bf16[128,512]{1,0:T(8,128)(2,1)S(1)}, bf16[128,512]{1,0:T(8,128)(2,1)S(1)}, u32[]{:S(2)}, u32[]{:S(2)}) %collective-permute-start.33) | collective-permute-done | bytes 131104 | tf_op jit(solution)/shard_map/ppermute | solution.py:178
  (88 shorter events, 42.1 us)
Async XLA Ops:
  0.0 10.8 %collective-permute-start.2 = (bf16[2,16,4096]{2,1,0:T(8,128)(2,1)}, bf16[2,16,4096]{2,1,0:T(8,128)(2,1)S(1)}, u32[]{:S(2)}, u32[]{:S(2)}) collective-permute-start(bf16[2,16,4096]{2,1,0:T(8,128)(2,1)} %bitcast.29), channel_id=1, source_target_pairs={{0,16},{4,20},{8,24},{12,28},{16,32},{20,36},{24,40},{28,44},{32,4... | collective-permute-start | bytes 786440 | tf_op jit(solution)/shard_map/ppermute | solution.py:40
  7.3 32.1 %collective-permute-start.13 = (bf16[4096,128]{1,0:T(8,128)(2,1)}, bf16[4096,128]{1,0:T(8,128)(2,1)}, u32[]{:S(2)}, u32[]{:S(2)}) collective-permute-start(bf16[4096,128]{1,0:T(8,128)(2,1)} %bitcast.26), channel_id=1, source_target_pairs={{0,64},{4,68},{8,72},{12,76},{16,80},{20,84},{24,88},{28,92},{32,9... | collective-permute-start | bytes 3145736 | tf_op jit(solution)/shard_map/ppermute | solution.py:164
  10.9 10.8 %collective-permute-start.6 = (bf16[3,16,4096]{2,1,0:T(8,128)(2,1)S(1)}, bf16[3,16,4096]{2,1,0:T(8,128)(2,1)S(1)}, u32[]{:S(2)}, u32[]{:S(2)}) collective-permute-start(bf16[3,16,4096]{2,1,0:T(8,128)(2,1)S(1)} %pad_maximum_fusion.7), channel_id=1, source_target_pairs={{0,16},{4,20},{8,24},{12,28},{16,32},{20,36},{24,40},{28,44},{32,4... | collective-permute-start | bytes 1179656 | tf_op jit(solution)/shard_map/ppermute | solution.py:40
  16.9 12.4 %collective-permute-start.5 = (bf16[3,16,4096]{2,1,0:T(8,128)(2,1)S(1)}, bf16[3,16,4096]{2,1,0:T(8,128)(2,1)S(1)}, u32[]{:S(2)}, u32[]{:S(2)}) collective-permute-start(bf16[3,16,4096]{2,1,0:T(8,128)(2,1)S(1)} %pad_maximum_fusion.6), channel_id=1, source_target_pairs={{0,12},{4,0},{8,4},{12,8},{16,28},{20,16},{24,20},{28,24},{32,44},... | collective-permute-start | bytes 1179656 | tf_op jit(solution)/shard_map/ppermute | solution.py:40
  21.7 11.5 %collective-permute-start.12 = (bf16[2,16,4096]{2,1,0:T(8,128)(2,1)S(1)}, bf16[2,16,4096]{2,1,0:T(8,128)(2,1)S(1)}, u32[]{:S(2)}, u32[]{:S(2)}) collective-permute-start(bf16[2,16,4096]{2,1,0:T(8,128)(2,1)S(1)} %bitcast.33), channel_id=1, source_target_pairs={{0,40},{4,44},{8,32},{12,36},{16,56},{20,60},{24,48},{28,52},{32,8... | collective-permute-start | bytes 786440 | tf_op jit(solution)/shard_map/ppermute | solution.py:57
  25.2 14.3 %collective-permute-start.10 = (bf16[2,16,4096]{2,1,0:T(8,128)(2,1)}, bf16[2,16,4096]{2,1,0:T(8,128)(2,1)S(1)}, u32[]{:S(2)}, u32[]{:S(2)}) collective-permute-start(bf16[2,16,4096]{2,1,0:T(8,128)(2,1)} %slice.118), channel_id=1, source_target_pairs={{0,16},{4,20},{8,24},{12,28},{16,32},{20,36},{24,40},{28,44},{32,4... | collective-permute-start | bytes 786440 | tf_op jit(solution)/shard_map/ppermute | solution.py:40
  26.1 13.3 %collective-permute-start.11 = (bf16[2,16,4096]{2,1,0:T(8,128)(2,1)}, bf16[2,16,4096]{2,1,0:T(8,128)(2,1)}, u32[]{:S(2)}, u32[]{:S(2)}) collective-permute-start(bf16[2,16,4096]{2,1,0:T(8,128)(2,1)} %slice.119), channel_id=1, source_target_pairs={{0,48},{4,52},{8,56},{12,60},{16,0},{20,4},{24,8},{28,12},{32,16},... | collective-permute-start | bytes 786440 | tf_op jit(solution)/shard_map/ppermute | solution.py:40
  29.3 10.2 %collective-permute-start.8 = (bf16[2,16,4096]{2,1,0:T(8,128)(2,1)}, bf16[2,16,4096]{2,1,0:T(8,128)(2,1)}, u32[]{:S(2)}, u32[]{:S(2)}) collective-permute-start(bf16[2,16,4096]{2,1,0:T(8,128)(2,1)} %slice.116), channel_id=1, source_target_pairs={{0,4},{4,8},{8,12},{12,0},{16,20},{20,24},{24,28},{28,16},{32,36},... | collective-permute-start | bytes 786440 | tf_op jit(solution)/shard_map/ppermute | solution.py:40
  52.8 10.0 %collective-permute-start.15 = (bf16[2,2,2,256,128]{4,3,2,1,0:T(8,128)(2,1)S(1)}, bf16[2,2,2,256,128]{4,3,2,1,0:T(8,128)(2,1)S(1)}, u32[]{:S(2)}, u32[]{:S(2)}) collective-permute-start(bf16[2,2,2,256,128]{4,3,2,1,0:T(8,128)(2,1)S(1)} %pad_maximum_fusion.4.refs_0_), channel_id=1, source_target_pairs={{0,4},{4,8},{8,12},{12,0},{16,20},{20,24},{24,28},{28,16},{32,36},... | collective-permute-start | bytes 1572872 | tf_op jit(solution)/shard_map/ppermute | solution.py:40
  55.0 10.3 %collective-permute-start.17 = (bf16[2,2,2,256,128]{4,3,2,1,0:T(8,128)(2,1)S(1)}, bf16[2,2,2,256,128]{4,3,2,1,0:T(8,128)(2,1)S(1)}, u32[]{:S(2)}, u32[]{:S(2)}) collective-permute-start(bf16[2,2,2,256,128]{4,3,2,1,0:T(8,128)(2,1)S(1)} %pad_maximum_fusion.4.refs_0_), channel_id=1, source_target_pairs={{0,16},{4,20},{8,24},{12,28},{16,32},{20,36},{24,40},{28,44},{32,4... | collective-permute-start | bytes 1572872 | tf_op jit(solution)/shard_map/ppermute | solution.py:40
  55.4 10.0 %collective-permute-start.16 = (bf16[2,2,2,256,128]{4,3,2,1,0:T(8,128)(2,1)S(1)}, bf16[2,2,2,256,128]{4,3,2,1,0:T(8,128)(2,1)S(1)}, u32[]{:S(2)}, u32[]{:S(2)}) collective-permute-start(bf16[2,2,2,256,128]{4,3,2,1,0:T(8,128)(2,1)S(1)} %pad_maximum_fusion.4.refs_0_), channel_id=1, source_target_pairs={{0,12},{4,0},{8,4},{12,8},{16,28},{20,16},{24,20},{28,24},{32,44},... | collective-permute-start | bytes 1572872 | tf_op jit(solution)/shard_map/ppermute | solution.py:40
  62.9 14.0 %collective-permute-start.22 = (bf16[3,2,2,256,128]{4,3,2,1,0:T(8,128)(2,1)S(1)}, bf16[3,2,2,256,128]{4,3,2,1,0:T(8,128)(2,1)S(1)}, u32[]{:S(2)}, u32[]{:S(2)}) collective-permute-start(bf16[3,2,2,256,128]{4,3,2,1,0:T(8,128)(2,1)S(1)} %pad_maximum_fusion.3), channel_id=1, source_target_pairs={{0,48},{4,52},{8,56},{12,60},{16,0},{20,4},{24,8},{28,12},{32,16},... | collective-permute-start | bytes 2359304 | tf_op jit(solution)/shard_map/ppermute | solution.py:40
  65.5 12.8 %collective-permute-start.21 = (bf16[3,2,2,256,128]{4,3,2,1,0:T(8,128)(2,1)S(1)}, bf16[3,2,2,256,128]{4,3,2,1,0:T(8,128)(2,1)S(1)}, u32[]{:S(2)}, u32[]{:S(2)}) collective-permute-start(bf16[3,2,2,256,128]{4,3,2,1,0:T(8,128)(2,1)S(1)} %pad_maximum_fusion.2), channel_id=1, source_target_pairs={{0,16},{4,20},{8,24},{12,28},{16,32},{20,36},{24,40},{28,44},{32,4... | collective-permute-start | bytes 2359304 | tf_op jit(solution)/shard_map/ppermute | solution.py:40
  65.7 20.6 %collective-permute-start.20 = (bf16[3,2,2,256,128]{4,3,2,1,0:T(8,128)(2,1)S(1)}, bf16[3,2,2,256,128]{4,3,2,1,0:T(8,128)(2,1)S(1)}, u32[]{:S(2)}, u32[]{:S(2)}) collective-permute-start(bf16[3,2,2,256,128]{4,3,2,1,0:T(8,128)(2,1)S(1)} %pad_maximum_fusion.1), channel_id=1, source_target_pairs={{0,12},{4,0},{8,4},{12,8},{16,28},{20,16},{24,20},{28,24},{32,44},... | collective-permute-start | bytes 2359304 | tf_op jit(solution)/shard_map/ppermute | solution.py:40
  66.3 23.4 %collective-permute-start.19 = (bf16[3,2,2,256,128]{4,3,2,1,0:T(8,128)(2,1)S(1)}, bf16[3,2,2,256,128]{4,3,2,1,0:T(8,128)(2,1)S(1)}, u32[]{:S(2)}, u32[]{:S(2)}) collective-permute-start(bf16[3,2,2,256,128]{4,3,2,1,0:T(8,128)(2,1)S(1)} %pad_maximum_fusion), channel_id=1, source_target_pairs={{0,4},{4,8},{8,12},{12,0},{16,20},{20,24},{24,28},{28,16},{32,36},... | collective-permute-start | bytes 2359304 | tf_op jit(solution)/shard_map/ppermute | solution.py:40
  67.4 23.0 %collective-permute-start.27 = (bf16[2,2,2,256,128]{4,3,2,1,0:T(8,128)(2,1)S(1)}, bf16[2,2,2,256,128]{4,3,2,1,0:T(8,128)(2,1)S(1)}, u32[]{:S(2)}, u32[]{:S(2)}) collective-permute-start(bf16[2,2,2,256,128]{4,3,2,1,0:T(8,128)(2,1)S(1)} %pad_maximum_fusion.4.refs_0_), channel_id=1, source_target_pairs={{0,40},{4,44},{8,32},{12,36},{16,56},{20,60},{24,48},{28,52},{32,8... | collective-permute-start | bytes 1572872 | tf_op jit(solution)/shard_map/ppermute | solution.py:57
  76.9 18.9 %collective-permute-start.26 = (bf16[2,2,2,256,128]{4,3,2,1,0:T(8,128)(2,1)S(1)}, bf16[2,2,2,256,128]{4,3,2,1,0:T(8,128)(2,1)S(1)}, u32[]{:S(2)}, u32[]{:S(2)}) collective-permute-start(bf16[2,2,2,256,128]{4,3,2,1,0:T(8,128)(2,1)S(1)} %slice.127), channel_id=1, source_target_pairs={{0,48},{4,52},{8,56},{12,60},{16,0},{20,4},{24,8},{28,12},{32,16},... | collective-permute-start | bytes 1572872 | tf_op jit(solution)/shard_map/ppermute | solution.py:40
  78.3 21.5 %collective-permute-start.25 = (bf16[2,2,2,256,128]{4,3,2,1,0:T(8,128)(2,1)S(1)}, bf16[2,2,2,256,128]{4,3,2,1,0:T(8,128)(2,1)S(1)}, u32[]{:S(2)}, u32[]{:S(2)}) collective-permute-start(bf16[2,2,2,256,128]{4,3,2,1,0:T(8,128)(2,1)S(1)} %slice.126), channel_id=1, source_target_pairs={{0,16},{4,20},{8,24},{12,28},{16,32},{20,36},{24,40},{28,44},{32,4... | collective-permute-start | bytes 1572872 | tf_op jit(solution)/shard_map/ppermute | solution.py:40
  86.2 18.6 %collective-permute-start.24 = (bf16[2,2,2,256,128]{4,3,2,1,0:T(8,128)(2,1)S(1)}, bf16[2,2,2,256,128]{4,3,2,1,0:T(8,128)(2,1)S(1)}, u32[]{:S(2)}, u32[]{:S(2)}) collective-permute-start(bf16[2,2,2,256,128]{4,3,2,1,0:T(8,128)(2,1)S(1)} %slice.125), channel_id=1, source_target_pairs={{0,12},{4,0},{8,4},{12,8},{16,28},{20,16},{24,20},{28,24},{32,44},... | collective-permute-start | bytes 1572872 | tf_op jit(solution)/shard_map/ppermute | solution.py:40
  89.8 17.2 %collective-permute-start.23 = (bf16[2,2,2,256,128]{4,3,2,1,0:T(8,128)(2,1)S(1)}, bf16[2,2,2,256,128]{4,3,2,1,0:T(8,128)(2,1)S(1)}, u32[]{:S(2)}, u32[]{:S(2)}) collective-permute-start(bf16[2,2,2,256,128]{4,3,2,1,0:T(8,128)(2,1)S(1)} %slice.124), channel_id=1, source_target_pairs={{0,4},{4,8},{8,12},{12,0},{16,20},{20,24},{24,28},{28,16},{32,36},... | collective-permute-start | bytes 1572872 | tf_op jit(solution)/shard_map/ppermute | solution.py:40
  120.6 15.2 %collective-permute-start.28 = (bf16[2,128,2048]{2,1,0:T(8,128)(2,1)S(1)}, bf16[2,128,2048]{2,1,0:T(8,128)(2,1)S(1)}, u32[]{:S(2)}, u32[]{:S(2)}) collective-permute-start(bf16[2,128,2048]{2,1,0:T(8,128)(2,1)S(1)} %get-tuple-element.16), channel_id=1, source_target_pairs={{0,1},{1,0},{2,3},{3,2},{4,5},{5,4},{6,7},{7,6},{8,9},{9,8},{10,11... | collective-permute-start | bytes 3145736 | tf_op jit(solution)/shard_map/ppermute | solution.py:174
  135.9 13.2 %collective-permute-start.29 = (bf16[128,2048]{1,0:T(8,128)(2,1)S(1)}, bf16[128,2048]{1,0:T(8,128)(2,1)S(1)}, u32[]{:S(2)}, u32[]{:S(2)}) collective-permute-start(bf16[128,2048]{1,0:T(8,128)(2,1)S(1)} %fusion), channel_id=1, source_target_pairs={{0,2},{2,0},{1,3},{3,1},{4,6},{6,4},{5,7},{7,5},{8,10},{10,8},{9,1... | collective-permute-start | bytes 1572872 | tf_op jit(solution)/shard_map/ppermute | solution.py:178
  156.9 13.7 %collective-permute-start.31 = (bf16[128,1536]{1,0:T(8,128)(2,1)S(1)}, bf16[128,1536]{1,0:T(8,128)(2,1)S(1)}, u32[]{:S(2)}, u32[]{:S(2)}) collective-permute-start(bf16[128,1536]{1,0:T(8,128)(2,1)S(1)} %fusion.1), channel_id=1, source_target_pairs={{0,2},{2,0},{1,3},{3,1},{4,6},{6,4},{5,7},{7,5},{8,10},{10,8},{9,1... | collective-permute-start | bytes 1179656 | tf_op jit(solution)/shard_map/ppermute | solution.py:178
  158.1 12.5 %collective-permute-start.33 = (bf16[128,512]{1,0:T(8,128)(2,1)S(1)}, bf16[128,512]{1,0:T(8,128)(2,1)S(1)}, u32[]{:S(2)}, u32[]{:S(2)}) collective-permute-start(bf16[128,512]{1,0:T(8,128)(2,1)S(1)} %fusion.2), channel_id=1, source_target_pairs={{0,2},{2,0},{1,3},{3,1},{4,6},{6,4},{5,7},{7,5},{8,10},{10,8},{9,1... | collective-permute-start | bytes 393224 | tf_op jit(solution)/shard_map/ppermute | solution.py:178
  (12 other events, 90.7 us)

commit v2 on v1

--- a/solution.py
+++ b/solution.py
@@ -13,7 +13,6 @@
 RA = 16 * SUB
 TT = 512
 NTL = 2048
-TILES = (((0, 4),), ((0, 3), (3, 1)))
 
 
 def perm_of(f):
@@ -29,7 +28,8 @@
 DOWN_Y = perm_of(lambda a, b, c: (a, b, c - 1))
 UP_Z = perm_of(lambda a, b, c: (a, b + 1, c))
 DOWN_Z = perm_of(lambda a, b, c: (a, b - 1, c))
-CORNER = perm_of(lambda a, b, c: (a, b + 2, c + 2))
+FAR_Y = perm_of(lambda a, b, c: (a, b, c + 2))
+FAR_Z = perm_of(lambda a, b, c: (a, b + 2, c))
 XH = perm_of(lambda a, b, c: (a + 1, b, c))
 CORE = [(0, 1), (1, 0), (2, 3), (3, 2)]
 XL = [(0, 2), (2, 0), (1, 3), (3, 1)]
@@ -53,12 +53,15 @@
     _, ly, ry, lz, rz = near
     cat = lambda a, b: jnp.concatenate([a, b], axis=0)
     two = send4(cat(lz, ly[:1]), cat(rz, ry[1:]), cat(ry, lz[:1]), cat(ly, rz[1:]))
+    corner0 = lax.ppermute(two[2][2], "rows", FAR_Y)
     three = send4(*[x[:2] for x in two])
-    return [*near, *two, *three, lax.ppermute(block, "rows", CORNER)]
+    corner1 = lax.ppermute(two[1][2], "rows", FAR_Z)
+    return [*near, *two, *three, corner0, corner1]
 
 
 def condition_kernel(pos, *refs):
-    near, two, three, (corner, own, other, out, q, p, sem) = refs[:5], refs[5:9], refs[9:13], refs[13:]
+    near, two, three, corner = refs[:5], refs[5:9], refs[9:13], refs[13:15]
+    own, other, out, q, p, sem = refs[15:]
     xh, z, y = pos[0], pos[1], pos[2]
     at = lambda d: ((z + d[0]) % 4) * 4 + (y + d[1]) % 4
     copies = [(own, p.at[:, pl.ds(pl.multiple_of(xh * COLS, COLS), COLS)])]
@@ -67,7 +70,7 @@
     copies += [(x.at[0:2], q.at[at(d)]) for x, d in zip(two, DIAGONAL)]
     copies += [(x.at[2], q.at[at(d), k % 2]) for k, (x, d) in enumerate(zip(two, FAR))]
     copies += [(x, q.at[at(d)]) for x, d in zip(three, KNIGHT)]
-    copies += [(corner, q.at[at((2, 2))])]
+    copies += [(x, q.at[at((2, 2)), k]) for k, x in enumerate(corner)]
     copies = [pltpu.make_async_copy(src, dst, sem.at[i]) for i, (src, dst) in enumerate(copies)]
     for c in copies:
         c.start()
@@ -84,12 +87,14 @@
     return pl.pallas_call(
         condition_kernel,
         out_shape=jax.ShapeDtypeStruct((2, 2, RA, COLS), jnp.bfloat16),
-        in_specs=[pl.BlockSpec(memory_space=pltpu.SMEM)] + [pl.BlockSpec(memory_space=pltpu.HBM)] * 16,
+        in_specs=[pl.BlockSpec(memory_space=pltpu.SMEM)]
+        + [pl.BlockSpec(memory_space=pltpu.HBM)] * 15
+        + [pl.BlockSpec(memory_space=pl.ANY)] * 2,
         out_specs=pl.BlockSpec(memory_space=pltpu.VMEM),
         scratch_shapes=[
             pltpu.VMEM((16, 2, SUB, F), jnp.bfloat16),
             pltpu.VMEM((F, 2 * COLS), jnp.bfloat16),
-            pltpu.SemaphoreType.DMA((20,)),
+            pltpu.SemaphoreType.DMA((21,)),
         ],
         compiler_params=pltpu.CompilerParams(vmem_limit_bytes=24 << 20),
         cost_estimate=pl.CostEstimate(flops=4 * RA * F * 256, bytes_accessed=6 << 20, transcendentals=0),
@@ -97,8 +102,95 @@
     )(pos, *pieces, own, other)
 
 
+def split(s, same, core, keep, send):
+    for i in range(2):
+        own = jnp.where(same, s[i], s[1 - i])
+        keep[i] = jnp.where(core == 0, own[0], own[1])
+        send[i] = jnp.where(core == 0, own[1], own[0]).astype(jnp.bfloat16)
+
+
+def near_blocks(chunk):
+    return [(k, chunk, d) for k, d in enumerate(NEAR)]
+
+
+def middle_blocks(chunk):
+    out = [(5 + k, chunk, d) for k, d in enumerate(DIAGONAL)]
+    return out + [(5 + k, 2, FAR[k]) for k in (chunk, 2 + chunk)]
+
+
+def last_blocks(chunk):
+    return [(9 + k, chunk, d) for k, d in enumerate(KNIGHT)] + [(13 + chunk, None, (2, 2))]
+
+
+def part_kernel(blocks, first, final, pos, *refs):
+    n = len(blocks)
+    arrays = sorted({k for k, _, _ in blocks})
+    pieces, cols, rest = refs[: len(arrays)], refs[len(arrays) : len(arrays) + 2 * n], refs[len(arrays) + 2 * n :]
+    c, sem = rest[-2:]
+
+    @pl.when(pl.program_id(0) == 0)
+    def _():
+        copies = [
+            pltpu.make_async_copy(
+                pieces[arrays.index(k)].at[i] if i is not None else pieces[arrays.index(k)],
+                c.at[:, :, :, j * COLS : (j + 1) * COLS], sem.at[j]
+            )
+            for j, (k, i, _) in enumerate(blocks)
+        ]
+        for x in copies:
+            x.start()
+        for x in copies:
+            x.wait()
+
+    lhs = jnp.concatenate([c[:, 0].reshape(2 * RA, n * COLS), c[:, 1].reshape(2 * RA, n * COLS)], axis=1)
+    rhs = jnp.concatenate([x[...] for x in cols], axis=1)
+    s = lax.dot_general(lhs, rhs, (((1,), (1,)), ((), ())), preferred_element_type=jnp.float32)
+    if not first:
+        s += rest[0][...]
+    if final:
+        split(s.reshape(2, 2, RA // 2, TT), pos[0] == pos[3], pos[4], *rest[-4:-2])
+    else:
+        rest[-3][...] = s
+
+
+def part(pos, pieces, train, blocks, acc=None, final=False, tiles=(0, NTL // TT)):
+    n = len(blocks)
+    arrays = sorted({k for k, _, _ in blocks})
+    skip, steps = tiles
+
+    def column(h, d):
+        return lambda i, p: (skip + i, h * 16 + lax.rem(p[1] + d[0], 4) * 4 + lax.rem(p[2] + d[1], 4))
+
+    in_specs = [pl.BlockSpec(memory_space=pltpu.HBM)] * len(arrays)
+    in_specs += [pl.BlockSpec((TT, COLS), column(h, d)) for h in range(2) for _, _, d in blocks]
+    if acc is not None:
+        in_specs.append(pl.BlockSpec((2 * RA, TT), lambda i, p: (0, skip + i)))
+    if final:
+        out_shape = tuple(jax.ShapeDtypeStruct((2, RA // 2, steps * TT), t) for t in (jnp.float32, jnp.bfloat16))
+        out_specs = (pl.BlockSpec((2, RA // 2, TT), lambda i, p: (0, 0, i)),) * 2
+    else:
+        out_shape = jax.ShapeDtypeStruct((2 * RA, NTL), jnp.float32)
+        out_specs = pl.BlockSpec((2 * RA, TT), lambda i, p: (0, i))
+    return pl.pallas_call(
+        functools.partial(part_kernel, blocks, acc is None, final),
+        grid_spec=pltpu.PrefetchScalarGridSpec(
+            num_scalar_prefetch=1,
+            grid=(steps,),
+            in_specs=in_specs,
+            out_specs=out_specs,
+            scratch_shapes=[pltpu.VMEM((2, 2, RA, n * COLS), jnp.bfloat16), pltpu.SemaphoreType.DMA((n,))],
+        ),
+        out_shape=out_shape,
+        compiler_params=pltpu.CompilerParams(vmem_limit_bytes=36 << 20),
+        cost_estimate=pl.CostEstimate(
+            flops=4 * RA * n * 2 * COLS * steps * TT, bytes_accessed=steps * TT * (n * 512 + RA * 16), transcendentals=0
+        ),
+        name="part",
+    )(pos, *[pieces[k] for k in arrays], *[train] * (2 * n), *([] if acc is None else [acc]))
+
+
 def score_kernel(chunk, pos, *refs):
-    near, two, three, (corner, t, keep, send, c, sem) = refs[:5], refs[5:9], refs[9:13], refs[13:]
+    near, two, three, corner, (t, keep, send, c, sem) = refs[:5], refs[5:9], refs[9:13], refs[13:15], refs[15:]
     xh, z, y, xl, core = (pos[i] for i in range(5))
 
     @pl.when(pl.program_id(0) == 0)
@@ -108,7 +200,7 @@
         copies += [(x.at[chunk], at(d)) for x, d in zip(two, DIAGONAL)]
         copies += [(two[k].at[2], at(FAR[k])) for k in (chunk, 2 + chunk)]
         copies += [(x.at[chunk], at(d)) for x, d in zip(three, KNIGHT)]
-        copies += [(corner.at[chunk], at((2, 2)))]
+        copies += [(corner[chunk], at((2, 2)))]
         copies = [pltpu.make_async_copy(src, dst, sem.at[i]) for i, (src, dst) in enumerate(copies)]
         for x in copies:
             x.start()
@@ -123,12 +215,7 @@
             (((1,), (1,)), ((), ())),
             preferred_element_type=jnp.float32,
         )
-    s = s.reshape(2, 2, RA // 2, TT)
-    same = xh == xl
-    for i in range(2):
-        own = jnp.where(same, s[i], s[1 - i])
-        keep[i] = jnp.where(core == 0, own[0], own[1])
-        send[i] = jnp.where(core == 0, own[1], own[0]).astype(jnp.bfloat16)
+    split(s.reshape(2, 2, RA // 2, TT), xh == xl, core, keep, send)
 
 
 def score(pos, pieces, train, chunk, first, steps):
@@ -140,7 +227,7 @@
             jax.ShapeDtypeStruct((2, RA // 2, steps * TT), jnp.bfloat16),
         ),
         in_specs=[pl.BlockSpec(memory_space=pltpu.SMEM)]
-        + [pl.BlockSpec(memory_space=pltpu.HBM)] * 14
+        + [pl.BlockSpec(memory_space=pltpu.HBM)] * 15
         + [pl.BlockSpec((TT, F), lambda i: (i + first, 0))],
         out_specs=(
             pl.BlockSpec((2, RA // 2, TT), lambda i: (0, 0, i)),
@@ -162,26 +249,31 @@
     p = precond.reshape(F, COLS)
     train = pltpu.with_memory_space_constraint(train_grads.reshape(NTL, F), pltpu.HBM)
     p_other = lax.ppermute(p, "rows", XH)
-
     cond = condition(pos, flood(q), p, p_other)
 
     partner = lax.ppermute(cond, "rows", XH)
     pieces = flood(jnp.stack([cond, partner], axis=1))
+    acc = part(pos, pieces, train, near_blocks(0))
+    acc = part(pos, pieces, train, middle_blocks(0), acc)
     out = jnp.zeros((8, 2, SUB, NTL), jnp.float32)
-    for chunk in range(2):
-        for first, steps in TILES[chunk]:
-            keep, send = score(pos, pieces, train, chunk, first, steps)
-            got = lax.ppermute(send, "layers", CORE)
-            away = (keep[1] + got[1].astype(jnp.float32)).astype(jnp.bfloat16)
-            if chunk == 0:
-                pos, away = lax.optimization_barrier((pos, away))
-            back = lax.ppermute(away, "layers", XL)
-            total = keep[0] + got[0].astype(jnp.float32) + back.astype(jnp.float32)
-            out = lax.dynamic_update_slice(out, total.reshape(8, 1, SUB, steps * TT), (0, chunk, 0, first * TT))
-            if chunk == 0:
-                pos_late, out = lax.optimization_barrier((pos, out))
-            elif first == 0:
-                pos = pos_late
+
+    def reduce(out, keep, send, chunk, first):
+        got = lax.ppermute(send, "layers", CORE)
+        away = (keep[1] + got[1].astype(jnp.float32)).astype(jnp.bfloat16)
+        back = lax.ppermute(away, "layers", XL)
+        total = keep[0] + got[0].astype(jnp.float32) + back.astype(jnp.float32)
+        width = total.shape[1]
+        return lax.dynamic_update_slice(out, total.reshape(8, 1, SUB, width), (0, chunk, 0, first * TT)), away, back
+
+    keep, send = part(pos, pieces, train, last_blocks(0), acc, True)
+    send, pieces[14] = lax.optimization_barrier((send, pieces[14]))
+    out, away, back = reduce(out, keep, send, 0, 0)
+    pos1, _ = lax.optimization_barrier((pos, away))
+    keep, send = score(pos1, pieces, train, 1, 0, 3)
+    send, _ = lax.optimization_barrier((send, back))
+    out, away, _ = reduce(out, keep, send, 1, 0)
+    pos2, _ = lax.optimization_barrier((pos1, away))
+    out, _, _ = reduce(out, *score(pos2, pieces, train, 1, 3, 1), 1, 3)
     return out.reshape(256, NTL)
 
 

time: 173 us -> 151 us (0.87)
  waiting for transfers between devices: 72 us -> 48.9 us
  starting transfers between devices: 57.7 us -> 49.4 us
  Pallas kernels: 35 us -> 43.1 us
    pallas_call x0 -> x3, Pallas kernels: none -> 21.8 us  [part(): pl.pallas_call(functools.partial(part_kernel, blocks, acc is None, final)...]
    ppermute x24, waiting for transfers between devices: 51.8 us -> 34.7 us  [send4(): lax.ppermute(x, 'rows', perm)]
    pallas_call x3 -> x2, Pallas kernels: 30.8 us -> 17.1 us  [score(): pl.pallas_call(functools.partial(score_kernel, chunk), grid=(steps,), out...]
    ppermute x8 -> x10, starting transfers between devices: 24.8 us -> 16.1 us  [the longest x3 8.88 us: reduce(): got = lax.ppermute(send, 'layers', CORE)]
    ppermute x8 -> x10, waiting for transfers between devices: 16.1 us -> 10.1 us  [the longest x3 5.08 us: reduce(): back = lax.ppermute(away, 'layers', XL)]
  transfers between devices with their start and end apart: 34 -> 36, of which waited for: 22 -> 19; matrix products, arithmetic and copies ran while one was open for 2% -> 3% of each run, Pallas kernels for 10% -> 26%
where the time goes in v2:
time: 151 us
  starting transfers between devices  49.4 us (33%)
  waiting for transfers between devices  48.9 us (32%)
  Pallas kernels  43.1 us (29%)
  local copies, waits for them, and re-layouts  7.88 us (5%)
    ppermute x24, waiting for transfers between devices, send4(): lax.ppermute(x, 'rows', perm)  34.7 us
    ppermute x24, starting transfers between devices, send4(): lax.ppermute(x, 'rows', perm)  27.8 us
    pallas_call x3, Pallas kernels, part(): pl.pallas_call(functools.partial(part_kernel, blocks, acc is None, final)...  21.8 us
    pallas_call x2, Pallas kernels, score(): pl.pallas_call(functools.partial(score_kernel, chunk), grid=(steps,), out...  17.1 us
    ppermute x3, starting transfers between devices, reduce(): got = lax.ppermute(send, 'layers', CORE)  8.88 us
    ppermute x3, waiting for transfers between devices, reduce(): back = lax.ppermute(away, 'layers', XL)  5.08 us
    ppermute x3, waiting for transfers between devices, reduce(): got = lax.ppermute(send, 'layers', CORE)  4.97 us
    pallas_call x1, Pallas kernels, condition(): pl.pallas_call(condition_kernel, out_shape=jax.ShapeDtypeStruct((2, 2, RA...  4.18 us
  transfers between devices with their start and end apart: 36, of which 19 were waited for; matrix products, arithmetic and copies ran while one was open for 3% of the time, Pallas kernels for 26%

profile of v2, /device:TPU:1, one launch (start us, length us, event | category | flops | bytes accessed | tf_op | source)
XLA Modules:
  0.0 150.7 jit_solution(11289510348402966305)
XLA Ops:
  0.0 2.5 %collective-permute-start.2 = (bf16[2,16,4096]{2,1,0:T(8,128)(2,1)}, bf16[2,16,4096]{2,1,0:T(8,128)(2,1)S(1)}, u32[]{:S(2)}, u32[]{:S(2)}) collective-permute-start(bf16[2,16,4096]{2,1,0:T(8,128)(2,1)} %bitcast.37), channel_id=1, source_target_pairs={{0,16},{4,20},{8,24},{12,28},{16,32},{20,36},{24,40},{28,44},{32,4... | collective-permute-start | bytes 786440 | tf_op jit(solution)/shard_map/ppermute | solution.py:40
  2.5 2.7 %collective-permute-start.1 = (bf16[2,16,4096]{2,1,0:T(8,128)(2,1)}, bf16[2,16,4096]{2,1,0:T(8,128)(2,1)S(1)}, u32[]{:S(2)}, u32[]{:S(2)}) collective-permute-start(bf16[2,16,4096]{2,1,0:T(8,128)(2,1)} %bitcast.38), channel_id=1, source_target_pairs={{0,12},{4,0},{8,4},{12,8},{16,28},{20,16},{24,20},{28,24},{32,44},... | collective-permute-start | bytes 786440 | tf_op jit(solution)/shard_map/ppermute | solution.py:40
  5.2 2.1 %collective-permute-start.3 = (bf16[2,16,4096]{2,1,0:T(8,128)(2,1)}, bf16[2,16,4096]{2,1,0:T(8,128)(2,1)S(1)}, u32[]{:S(2)}, u32[]{:S(2)}) collective-permute-start(bf16[2,16,4096]{2,1,0:T(8,128)(2,1)} %bitcast.39), channel_id=1, source_target_pairs={{0,48},{4,52},{8,56},{12,60},{16,0},{20,4},{24,8},{28,12},{32,16},... | collective-permute-start | bytes 786440 | tf_op jit(solution)/shard_map/ppermute | solution.py:40
  7.3 2.7 %collective-permute-start.14 = (bf16[4096,128]{1,0:T(8,128)(2,1)}, bf16[4096,128]{1,0:T(8,128)(2,1)}, u32[]{:S(2)}, u32[]{:S(2)}) collective-permute-start(bf16[4096,128]{1,0:T(8,128)(2,1)} %bitcast.34), channel_id=1, source_target_pairs={{0,64},{4,68},{8,72},{12,76},{16,80},{20,84},{24,88},{28,92},{32,9... | collective-permute-start | bytes 3145736 | tf_op jit(solution)/shard_map/ppermute | solution.py:251
  12.4 2.9 %collective-permute-start.5 = (bf16[3,16,4096]{2,1,0:T(8,128)(2,1)S(1)}, bf16[3,16,4096]{2,1,0:T(8,128)(2,1)S(1)}, u32[]{:S(2)}, u32[]{:S(2)}) collective-permute-start(bf16[3,16,4096]{2,1,0:T(8,128)(2,1)S(1)} %pad_maximum_fusion.6), channel_id=1, source_target_pairs={{0,12},{4,0},{8,4},{12,8},{16,28},{20,16},{24,20},{28,24},{32,44},... | collective-permute-start | bytes 1179656 | tf_op jit(solution)/shard_map/ppermute | solution.py:40
  17.6 4.1 %collective-permute-done.6.refs_7_ = bf16[3,16,4096]{2,1,0:T(8,128)(2,1)S(1)} collective-permute-done((bf16[3,16,4096]{2,1,0:T(8,128)(2,1)S(1)}, bf16[3,16,4096]{2,1,0:T(8,128)(2,1)S(1)}, u32[]{:S(2)}, u32[]{:S(2)}) %collective-permute-start.6) | collective-permute-done | bytes 393248 | tf_op jit(solution)/shard_map/ppermute | solution.py:40
  21.7 3.0 %collective-permute-start.12 = (bf16[16,4096]{1,0:T(8,128)(2,1)S(1)}, bf16[16,4096]{1,0:T(8,128)(2,1)S(1)}, u32[]{:S(2)}, u32[]{:S(2)}) collective-permute-start(bf16[16,4096]{1,0:T(8,128)(2,1)S(1)} %slice_bitcast_fusion.3), channel_id=1, source_target_pairs={{0,8},{4,12},{8,0},{12,4},{16,24},{20,28},{24,16},{28,20},{32,40},... | collective-permute-start | bytes 393224 | tf_op jit(solution)/shard_map/ppermute | solution.py:56
  30.4 2.7 %collective-permute-start.11 = (bf16[2,16,4096]{2,1,0:T(8,128)(2,1)}, bf16[2,16,4096]{2,1,0:T(8,128)(2,1)}, u32[]{:S(2)}, u32[]{:S(2)}) collective-permute-start(bf16[2,16,4096]{2,1,0:T(8,128)(2,1)} %slice.135), channel_id=1, source_target_pairs={{0,48},{4,52},{8,56},{12,60},{16,0},{20,4},{24,8},{28,12},{32,16},... | collective-permute-start | bytes 786440 | tf_op jit(solution)/shard_map/ppermute | solution.py:40
  36.7 3.8 %collective-permute-done.8.refs_9_ = bf16[2,16,4096]{2,1,0:T(8,128)(2,1)} collective-permute-done((bf16[2,16,4096]{2,1,0:T(8,128)(2,1)}, bf16[2,16,4096]{2,1,0:T(8,128)(2,1)}, u32[]{:S(2)}, u32[]{:S(2)}) %collective-permute-start.8) | collective-permute-done | bytes 262176 | tf_op jit(solution)/shard_map/ppermute | solution.py:40
  42.7 4.2 %condition.1 = bf16[2,2,256,128]{3,2,1,0:T(8,128)(2,1)S(1)} custom-call(s32[5]{0:T(128)S(1)} %stack.32.pos, bf16[2,16,4096]{2,1,0:T(8,128)(2,1)S(1)} %bitcast.41, bf16[2,16,4096]{2,1,0:T(8,128)(2,1)S(1)} %collective-permute-done.refs_1_, bf16[2,16,4096]{2,1,0:T(8,128)(2,1)S(1)} %collective-permute-done.1.refs_2_, ...), custom_call_target="tpu_custom_call" | custom-call | flops 1073741824 | bytes 6291456 | tf_op jit(solution)/shard_map/condition/pallas_call | solution.py:87
  46.8 2.7 %collective-permute-start.15 = (bf16[2,2,256,128]{3,2,1,0:T(8,128)(2,1)S(1)}, bf16[2,2,256,128]{3,2,1,0:T(8,128)(2,1)S(1)}, u32[]{:S(2)}, u32[]{:S(2)}) collective-permute-start(bf16[2,2,256,128]{3,2,1,0:T(8,128)(2,1)S(1)} %condition.1), channel_id=1, source_target_pairs={{0,64},{4,68},{8,72},{12,76},{16,80},{20,84},{24,88},{28,92},{32,9... | collective-permute-start | bytes 786440 | tf_op jit(solution)/shard_map/ppermute | solution.py:254
  49.6 4.1 %collective-permute-done.15 = bf16[2,2,256,128]{3,2,1,0:T(8,128)(2,1)S(1)} collective-permute-done((bf16[2,2,256,128]{3,2,1,0:T(8,128)(2,1)S(1)}, bf16[2,2,256,128]{3,2,1,0:T(8,128)(2,1)S(1)}, u32[]{:S(2)}, u32[]{:S(2)}) %collective-permute-start.15) | collective-permute-done | bytes 262176 | tf_op jit(solution)/shard_map/ppermute | solution.py:254
  53.9 2.6 %collective-permute-start.20 = (bf16[2,2,2,256,128]{4,3,2,1,0:T(8,128)(2,1)S(1)}, bf16[2,2,2,256,128]{4,3,2,1,0:T(8,128)(2,1)S(1)}, u32[]{:S(2)}, u32[]{:S(2)}) collective-permute-start(bf16[2,2,2,256,128]{4,3,2,1,0:T(8,128)(2,1)S(1)} %pad_maximum_fusion.4.refs_0_), channel_id=1, source_target_pairs={{0,48},{4,52},{8,56},{12,60},{16,0},{20,4},{24,8},{28,12},{32,16},... | collective-permute-start | bytes 1572872 | tf_op jit(solution)/shard_map/ppermute | solution.py:40
  57.9 5.1 %collective-permute-done.16.refs_3_ = bf16[2,2,2,256,128]{4,3,2,1,0:T(8,128)(2,1)S(1)} collective-permute-done((bf16[2,2,2,256,128]{4,3,2,1,0:T(8,128)(2,1)S(1)}, bf16[2,2,2,256,128]{4,3,2,1,0:T(8,128)(2,1)S(1)}, u32[]{:S(2)}, u32[]{:S(2)}) %collective-permute-start.16) | collective-permute-done | bytes 524320 | tf_op jit(solution)/shard_map/ppermute | solution.py:40
  63.2 2.7 %collective-permute-done.17.refs_1_ = bf16[2,2,2,256,128]{4,3,2,1,0:T(8,128)(2,1)S(1)} collective-permute-done((bf16[2,2,2,256,128]{4,3,2,1,0:T(8,128)(2,1)S(1)}, bf16[2,2,2,256,128]{4,3,2,1,0:T(8,128)(2,1)S(1)}, u32[]{:S(2)}, u32[]{:S(2)}) %collective-permute-start.17) | collective-permute-done | bytes 524320 | tf_op jit(solution)/shard_map/ppermute | solution.py:40
  68.0 11.1 %collective-permute-done.24.refs_2_.refs_7_ = bf16[3,2,2,256,128]{4,3,2,1,0:T(8,128)(2,1)S(1)} collective-permute-done((bf16[3,2,2,256,128]{4,3,2,1,0:T(8,128)(2,1)S(1)}, bf16[3,2,2,256,128]{4,3,2,1,0:T(8,128)(2,1)S(1)}, u32[]{:S(2)}, u32[]{:S(2)}) %collective-permute-start.24) | collective-permute-done | bytes 786464 | tf_op jit(solution)/shard_map/ppermute | solution.py:40
  79.3 6.9 %part.3.refs_16_ = f32[512,2048]{1,0:T(8,128)S(1)} custom-call(s32[5]{0:T(128)S(1)} %stack.32.pos, bf16[2,2,2,256,128]{4,3,2,1,0:T(8,128)(2,1)S(1)} %pad_maximum_fusion.4.refs_0_, bf16[2,2,2,256,128]{4,3,2,1,0:T(8,128)(2,1)S(1)} %collective-permute-done.17.refs_1_, bf16[2,2,2,256,128]{4,3,2,1,0:T(8,128)(2,1)S(1)} %collective-permute-done.21.refs_2_, ...), custom_call_target="tpu_custom_call" | custom-call | flops 2684354560 | bytes 13631488 | tf_op jit(solution)/shard_map/part/pallas_call | solution.py:174
  90.3 7.8 %part.4.refs_15_ = f32[512,2048]{1,0:T(8,128)S(1)} custom-call(s32[5]{0:T(128)S(1)} %stack.32.pos, bf16[3,2,2,256,128]{4,3,2,1,0:T(8,128)(2,1)S(1)} %collective-permute-done.18.refs_0_.refs_5_, bf16[3,2,2,256,128]{4,3,2,1,0:T(8,128)(2,1)S(1)} %collective-permute-done.22.refs_1_.refs_6_, ...), custom_call_target="tpu_custom_call" | custom-call | flops 3221225472 | bytes 14680064 | tf_op jit(solution)/shard_map/part/pallas_call | solution.py:174
  101.9 7.1 %part.5 = (f32[2,128,2048]{2,1,0:T(8,128)S(1)}, bf16[2,128,2048]{2,1,0:T(8,128)(2,1)S(1)}) custom-call(s32[5]{0:T(128)S(1)} %stack.32.pos, bf16[2,2,2,256,128]{4,3,2,1,0:T(8,128)(2,1)S(1)} %collective-permute-done.19.refs_0_.refs_9_, bf16[2,2,2,256,128]{4,3,2,1,0:T(8,128)(2,1)S(1)} %collective-permute-done.23.refs_1_.refs_10_, ...), custom_call_target="tpu_custom_call" | custom-call | flops 2684354560 | bytes 13631488 | tf_op jit(solution)/shard_map/part/pallas_call | solution.py:174
  109.1 7.0 %collective-permute-start.30 = (bf16[2,128,2048]{2,1,0:T(8,128)(2,1)S(1)}, bf16[2,128,2048]{2,1,0:T(8,128)(2,1)S(1)}, u32[]{:S(2)}, u32[]{:S(2)}) collective-permute-start(bf16[2,128,2048]{2,1,0:T(8,128)(2,1)S(1)} %get-tuple-element.18), channel_id=1, source_target_pairs={{0,1},{1,0},{2,3},{3,2},{4,5},{5,4},{6,7},{7,6},{8,9},{9,8},{10,11... | collective-permute-start | bytes 3145736 | tf_op jit(solution)/shard_map/ppermute | solution.py:261
  116.0 2.3 %collective-permute-done.30 = bf16[2,128,2048]{2,1,0:T(8,128)(2,1)S(1)} collective-permute-done((bf16[2,128,2048]{2,1,0:T(8,128)(2,1)S(1)}, bf16[2,128,2048]{2,1,0:T(8,128)(2,1)S(1)}, u32[]{:S(2)}, u32[]{:S(2)}) %collective-permute-start.30) | collective-permute-done | bytes 1048608 | tf_op jit(solution)/shard_map/ppermute | solution.py:261
  119.7 11.1 %score.2 = (f32[2,128,1536]{2,1,0:T(8,128)S(1)}, bf16[2,128,1536]{2,1,0:T(8,128)(2,1)S(1)}) custom-call(s32[5]{0:T(128)S(1)} %stack.32.pos, bf16[2,2,2,256,128]{4,3,2,1,0:T(8,128)(2,1)S(1)} %pad_maximum_fusion.4.refs_0_, bf16[2,2,2,256,128]{4,3,2,1,0:T(8,128)(2,1)S(1)} %collective-permute-done.17.refs_1_, ...), custom_call_target="tpu_custom_call" | custom-call | flops 6442450944 | bytes 16777216 | tf_op jit(solution)/shard_map/score/pallas_call | solution.py:222
  136.3 6.0 %score.3 = (f32[2,128,512]{2,1,0:T(8,128)S(1)}, bf16[2,128,512]{2,1,0:T(8,128)(2,1)S(1)}) custom-call(s32[5]{0:T(128)S(1)} %stack.32.pos, bf16[2,2,2,256,128]{4,3,2,1,0:T(8,128)(2,1)S(1)} %pad_maximum_fusion.4.refs_0_, bf16[2,2,2,256,128]{4,3,2,1,0:T(8,128)(2,1)S(1)} %collective-permute-done.17.refs_1_, ...), custom_call_target="tpu_custom_call" | custom-call | flops 2147483648 | bytes 8388608 | tf_op jit(solution)/shard_map/score/pallas_call | solution.py:222
  145.6 3.4 %collective-permute-done.35 = bf16[128,512]{1,0:T(8,128)(2,1)S(1)} collective-permute-done((bf16[128,512]{1,0:T(8,128)(2,1)S(1)}, bf16[128,512]{1,0:T(8,128)(2,1)S(1)}, u32[]{:S(2)}, u32[]{:S(2)}) %collective-permute-start.35) | collective-permute-done | bytes 131104 | tf_op jit(solution)/shard_map/ppermute | solution.py:263
  (102 shorter events, 39.7 us)
Async XLA Ops:
  0.0 10.8 %collective-permute-start.2 = (bf16[2,16,4096]{2,1,0:T(8,128)(2,1)}, bf16[2,16,4096]{2,1,0:T(8,128)(2,1)S(1)}, u32[]{:S(2)}, u32[]{:S(2)}) collective-permute-start(bf16[2,16,4096]{2,1,0:T(8,128)(2,1)} %bitcast.37), channel_id=1, source_target_pairs={{0,16},{4,20},{8,24},{12,28},{16,32},{20,36},{24,40},{28,44},{32,4... | collective-permute-start | bytes 786440 | tf_op jit(solution)/shard_map/ppermute | solution.py:40
  7.3 33.2 %collective-permute-start.14 = (bf16[4096,128]{1,0:T(8,128)(2,1)}, bf16[4096,128]{1,0:T(8,128)(2,1)}, u32[]{:S(2)}, u32[]{:S(2)}) collective-permute-start(bf16[4096,128]{1,0:T(8,128)(2,1)} %bitcast.34), channel_id=1, source_target_pairs={{0,64},{4,68},{8,72},{12,76},{16,80},{20,84},{24,88},{28,92},{32,9... | collective-permute-start | bytes 3145736 | tf_op jit(solution)/shard_map/ppermute | solution.py:251
  10.9 10.8 %collective-permute-start.6 = (bf16[3,16,4096]{2,1,0:T(8,128)(2,1)S(1)}, bf16[3,16,4096]{2,1,0:T(8,128)(2,1)S(1)}, u32[]{:S(2)}, u32[]{:S(2)}) collective-permute-start(bf16[3,16,4096]{2,1,0:T(8,128)(2,1)S(1)} %pad_maximum_fusion.7), channel_id=1, source_target_pairs={{0,16},{4,20},{8,24},{12,28},{16,32},{20,36},{24,40},{28,44},{32,4... | collective-permute-start | bytes 1179656 | tf_op jit(solution)/shard_map/ppermute | solution.py:40
  12.4 12.2 %collective-permute-start.5 = (bf16[3,16,4096]{2,1,0:T(8,128)(2,1)S(1)}, bf16[3,16,4096]{2,1,0:T(8,128)(2,1)S(1)}, u32[]{:S(2)}, u32[]{:S(2)}) collective-permute-start(bf16[3,16,4096]{2,1,0:T(8,128)(2,1)S(1)} %pad_maximum_fusion.6), channel_id=1, source_target_pairs={{0,12},{4,0},{8,4},{12,8},{16,28},{20,16},{24,20},{28,24},{32,44},... | collective-permute-start | bytes 1179656 | tf_op jit(solution)/shard_map/ppermute | solution.py:40
  15.5 10.9 %collective-permute-start.7 = (bf16[3,16,4096]{2,1,0:T(8,128)(2,1)S(1)}, bf16[3,16,4096]{2,1,0:T(8,128)(2,1)S(1)}, u32[]{:S(2)}, u32[]{:S(2)}) collective-permute-start(bf16[3,16,4096]{2,1,0:T(8,128)(2,1)S(1)} %pad_maximum_fusion.8), channel_id=1, source_target_pairs={{0,48},{4,52},{8,56},{12,60},{16,0},{20,4},{24,8},{28,12},{32,16},... | collective-permute-start | bytes 1179656 | tf_op jit(solution)/shard_map/ppermute | solution.py:40
  16.8 10.8 %collective-permute-start.4 = (bf16[3,16,4096]{2,1,0:T(8,128)(2,1)S(1)}, bf16[3,16,4096]{2,1,0:T(8,128)(2,1)S(1)}, u32[]{:S(2)}, u32[]{:S(2)}) collective-permute-start(bf16[3,16,4096]{2,1,0:T(8,128)(2,1)S(1)} %pad_maximum_fusion.5), channel_id=1, source_target_pairs={{0,4},{4,8},{8,12},{12,0},{16,20},{20,24},{24,28},{28,16},{32,36},... | collective-permute-start | bytes 1179656 | tf_op jit(solution)/shard_map/ppermute | solution.py:40
  21.7 8.8 %collective-permute-start.12 = (bf16[16,4096]{1,0:T(8,128)(2,1)S(1)}, bf16[16,4096]{1,0:T(8,128)(2,1)S(1)}, u32[]{:S(2)}, u32[]{:S(2)}) collective-permute-start(bf16[16,4096]{1,0:T(8,128)(2,1)S(1)} %slice_bitcast_fusion.3), channel_id=1, source_target_pairs={{0,8},{4,12},{8,0},{12,4},{16,24},{20,28},{24,16},{28,20},{32,40},... | collective-permute-start | bytes 393224 | tf_op jit(solution)/shard_map/ppermute | solution.py:56
  53.7 9.3 %collective-permute-start.16 = (bf16[2,2,2,256,128]{4,3,2,1,0:T(8,128)(2,1)S(1)}, bf16[2,2,2,256,128]{4,3,2,1,0:T(8,128)(2,1)S(1)}, u32[]{:S(2)}, u32[]{:S(2)}) collective-permute-start(bf16[2,2,2,256,128]{4,3,2,1,0:T(8,128)(2,1)S(1)} %pad_maximum_fusion.4.refs_0_), channel_id=1, source_target_pairs={{0,16},{4,20},{8,24},{12,28},{16,32},{20,36},{24,40},{28,44},{32,4... | collective-permute-start | bytes 1572872 | tf_op jit(solution)/shard_map/ppermute | solution.py:40
  53.8 9.3 %collective-permute-start.21 = (bf16[2,2,2,256,128]{4,3,2,1,0:T(8,128)(2,1)S(1)}, bf16[2,2,2,256,128]{4,3,2,1,0:T(8,128)(2,1)S(1)}, u32[]{:S(2)}, u32[]{:S(2)}) collective-permute-start(bf16[2,2,2,256,128]{4,3,2,1,0:T(8,128)(2,1)S(1)} %pad_maximum_fusion.4.refs_0_), channel_id=1, source_target_pairs={{0,12},{4,0},{8,4},{12,8},{16,28},{20,16},{24,20},{28,24},{32,44},... | collective-permute-start | bytes 1572872 | tf_op jit(solution)/shard_map/ppermute | solution.py:40
  53.9 9.3 %collective-permute-start.20 = (bf16[2,2,2,256,128]{4,3,2,1,0:T(8,128)(2,1)S(1)}, bf16[2,2,2,256,128]{4,3,2,1,0:T(8,128)(2,1)S(1)}, u32[]{:S(2)}, u32[]{:S(2)}) collective-permute-start(bf16[2,2,2,256,128]{4,3,2,1,0:T(8,128)(2,1)S(1)} %pad_maximum_fusion.4.refs_0_), channel_id=1, source_target_pairs={{0,48},{4,52},{8,56},{12,60},{16,0},{20,4},{24,8},{28,12},{32,16},... | collective-permute-start | bytes 1572872 | tf_op jit(solution)/shard_map/ppermute | solution.py:40
  56.5 9.5 %collective-permute-start.17 = (bf16[2,2,2,256,128]{4,3,2,1,0:T(8,128)(2,1)S(1)}, bf16[2,2,2,256,128]{4,3,2,1,0:T(8,128)(2,1)S(1)}, u32[]{:S(2)}, u32[]{:S(2)}) collective-permute-start(bf16[2,2,2,256,128]{4,3,2,1,0:T(8,128)(2,1)S(1)} %pad_maximum_fusion.4.refs_0_), channel_id=1, source_target_pairs={{0,4},{4,8},{8,12},{12,0},{16,20},{20,24},{24,28},{28,16},{32,36},... | collective-permute-start | bytes 1572872 | tf_op jit(solution)/shard_map/ppermute | solution.py:40
  63.1 15.9 %collective-permute-start.24 = (bf16[3,2,2,256,128]{4,3,2,1,0:T(8,128)(2,1)S(1)}, bf16[3,2,2,256,128]{4,3,2,1,0:T(8,128)(2,1)S(1)}, u32[]{:S(2)}, u32[]{:S(2)}) collective-permute-start(bf16[3,2,2,256,128]{4,3,2,1,0:T(8,128)(2,1)S(1)} %pad_maximum_fusion.2), channel_id=1, source_target_pairs={{0,16},{4,20},{8,24},{12,28},{16,32},{20,36},{24,40},{28,44},{32,4... | collective-permute-start | bytes 2359304 | tf_op jit(solution)/shard_map/ppermute | solution.py:40
  66.1 20.1 %collective-permute-start.26 = (bf16[3,2,2,256,128]{4,3,2,1,0:T(8,128)(2,1)S(1)}, bf16[3,2,2,256,128]{4,3,2,1,0:T(8,128)(2,1)S(1)}, u32[]{:S(2)}, u32[]{:S(2)}) collective-permute-start(bf16[3,2,2,256,128]{4,3,2,1,0:T(8,128)(2,1)S(1)} %pad_maximum_fusion.3), channel_id=1, source_target_pairs={{0,48},{4,52},{8,56},{12,60},{16,0},{20,4},{24,8},{28,12},{32,16},... | collective-permute-start | bytes 2359304 | tf_op jit(solution)/shard_map/ppermute | solution.py:40
  66.3 21.7 %collective-permute-start.22 = (bf16[3,2,2,256,128]{4,3,2,1,0:T(8,128)(2,1)S(1)}, bf16[3,2,2,256,128]{4,3,2,1,0:T(8,128)(2,1)S(1)}, u32[]{:S(2)}, u32[]{:S(2)}) collective-permute-start(bf16[3,2,2,256,128]{4,3,2,1,0:T(8,128)(2,1)S(1)} %pad_maximum_fusion.1), channel_id=1, source_target_pairs={{0,12},{4,0},{8,4},{12,8},{16,28},{20,16},{24,20},{28,24},{32,44},... | collective-permute-start | bytes 2359304 | tf_op jit(solution)/shard_map/ppermute | solution.py:40
  66.4 23.0 %collective-permute-start.18 = (bf16[3,2,2,256,128]{4,3,2,1,0:T(8,128)(2,1)S(1)}, bf16[3,2,2,256,128]{4,3,2,1,0:T(8,128)(2,1)S(1)}, u32[]{:S(2)}, u32[]{:S(2)}) collective-permute-start(bf16[3,2,2,256,128]{4,3,2,1,0:T(8,128)(2,1)S(1)} %pad_maximum_fusion), channel_id=1, source_target_pairs={{0,4},{4,8},{8,12},{12,0},{16,20},{20,24},{24,28},{28,16},{32,36},... | collective-permute-start | bytes 2359304 | tf_op jit(solution)/shard_map/ppermute | solution.py:40
  79.0 10.6 %collective-permute-start.28 = (bf16[2,2,256,128]{3,2,1,0:T(8,128)(2,1)S(1)}, bf16[2,2,256,128]{3,2,1,0:T(8,128)(2,1)S(1)}, u32[]{:S(2)}, u32[]{:S(2)}) collective-permute-start(bf16[2,2,256,128]{3,2,1,0:T(8,128)(2,1)S(1)} %slice_bitcast_fusion.1), channel_id=1, source_target_pairs={{0,8},{4,12},{8,0},{12,4},{16,24},{20,28},{24,16},{28,20},{32,40},... | collective-permute-start | bytes 786440 | tf_op jit(solution)/shard_map/ppermute | solution.py:56
  86.3 11.8 %collective-permute-start.27 = (bf16[2,2,2,256,128]{4,3,2,1,0:T(8,128)(2,1)S(1)}, bf16[2,2,2,256,128]{4,3,2,1,0:T(8,128)(2,1)S(1)}, u32[]{:S(2)}, u32[]{:S(2)}) collective-permute-start(bf16[2,2,2,256,128]{4,3,2,1,0:T(8,128)(2,1)S(1)} %slice.145), channel_id=1, source_target_pairs={{0,48},{4,52},{8,56},{12,60},{16,0},{20,4},{24,8},{28,12},{32,16},... | collective-permute-start | bytes 1572872 | tf_op jit(solution)/shard_map/ppermute | solution.py:40
  87.2 12.4 %collective-permute-start.25 = (bf16[2,2,2,256,128]{4,3,2,1,0:T(8,128)(2,1)S(1)}, bf16[2,2,2,256,128]{4,3,2,1,0:T(8,128)(2,1)S(1)}, u32[]{:S(2)}, u32[]{:S(2)}) collective-permute-start(bf16[2,2,2,256,128]{4,3,2,1,0:T(8,128)(2,1)S(1)} %slice.143), channel_id=1, source_target_pairs={{0,16},{4,20},{8,24},{12,28},{16,32},{20,36},{24,40},{28,44},{32,4... | collective-permute-start | bytes 1572872 | tf_op jit(solution)/shard_map/ppermute | solution.py:40
  87.9 12.3 %collective-permute-start.23 = (bf16[2,2,2,256,128]{4,3,2,1,0:T(8,128)(2,1)S(1)}, bf16[2,2,2,256,128]{4,3,2,1,0:T(8,128)(2,1)S(1)}, u32[]{:S(2)}, u32[]{:S(2)}) collective-permute-start(bf16[2,2,2,256,128]{4,3,2,1,0:T(8,128)(2,1)S(1)} %slice.141), channel_id=1, source_target_pairs={{0,12},{4,0},{8,4},{12,8},{16,28},{20,16},{24,20},{28,24},{32,44},... | collective-permute-start | bytes 1572872 | tf_op jit(solution)/shard_map/ppermute | solution.py:40
  89.5 12.4 %collective-permute-start.19 = (bf16[2,2,2,256,128]{4,3,2,1,0:T(8,128)(2,1)S(1)}, bf16[2,2,2,256,128]{4,3,2,1,0:T(8,128)(2,1)S(1)}, u32[]{:S(2)}, u32[]{:S(2)}) collective-permute-start(bf16[2,2,2,256,128]{4,3,2,1,0:T(8,128)(2,1)S(1)} %slice.139), channel_id=1, source_target_pairs={{0,4},{4,8},{8,12},{12,0},{16,20},{20,24},{24,28},{28,16},{32,36},... | collective-permute-start | bytes 1572872 | tf_op jit(solution)/shard_map/ppermute | solution.py:40
  89.6 19.4 %collective-permute-start.29 = (bf16[2,2,256,128]{3,2,1,0:T(8,128)(2,1)S(1)}, bf16[2,2,256,128]{3,2,1,0:T(8,128)(2,1)S(1)}, u32[]{:S(2)}, u32[]{:S(2)}) collective-permute-start(bf16[2,2,256,128]{3,2,1,0:T(8,128)(2,1)S(1)} %slice_bitcast_fusion), channel_id=1, source_target_pairs={{0,32},{4,36},{8,40},{12,44},{16,48},{20,52},{24,56},{28,60},{32,0... | collective-permute-start | bytes 786440 | tf_op jit(solution)/shard_map/ppermute | solution.py:58
  109.1 9.2 %collective-permute-start.30 = (bf16[2,128,2048]{2,1,0:T(8,128)(2,1)S(1)}, bf16[2,128,2048]{2,1,0:T(8,128)(2,1)S(1)}, u32[]{:S(2)}, u32[]{:S(2)}) collective-permute-start(bf16[2,128,2048]{2,1,0:T(8,128)(2,1)S(1)} %get-tuple-element.18), channel_id=1, source_target_pairs={{0,1},{1,0},{2,3},{3,2},{4,5},{5,4},{6,7},{7,6},{8,9},{9,8},{10,11... | collective-permute-start | bytes 3145736 | tf_op jit(solution)/shard_map/ppermute | solution.py:261
  118.4 13.2 %collective-permute-start.31 = (bf16[128,2048]{1,0:T(8,128)(2,1)S(1)}, bf16[128,2048]{1,0:T(8,128)(2,1)S(1)}, u32[]{:S(2)}, u32[]{:S(2)}) collective-permute-start(bf16[128,2048]{1,0:T(8,128)(2,1)S(1)} %fusion), channel_id=1, source_target_pairs={{0,2},{2,0},{1,3},{3,1},{4,6},{6,4},{5,7},{7,5},{8,10},{10,8},{9,1... | collective-permute-start | bytes 1572872 | tf_op jit(solution)/shard_map/ppermute | solution.py:263
  134.8 10.6 %collective-permute-start.33 = (bf16[128,1536]{1,0:T(8,128)(2,1)S(1)}, bf16[128,1536]{1,0:T(8,128)(2,1)S(1)}, u32[]{:S(2)}, u32[]{:S(2)}) collective-permute-start(bf16[128,1536]{1,0:T(8,128)(2,1)S(1)} %fusion.1), channel_id=1, source_target_pairs={{0,2},{2,0},{1,3},{3,1},{4,6},{6,4},{5,7},{7,5},{8,10},{10,8},{9,1... | collective-permute-start | bytes 1179656 | tf_op jit(solution)/shard_map/ppermute | solution.py:263
  (16 other events, 105.5 us)

commit v3 on v2

--- a/solution.py
+++ b/solution.py
@@ -3,6 +3,7 @@
 import jax
 import jax.numpy as jnp
 from jax import lax
+from jax.experimental.layout import Layout, with_layout_constraint
 from jax.experimental import pallas as pl
 from jax.experimental.pallas import tpu as pltpu
 from jax.sharding import PartitionSpec as P
@@ -215,10 +216,10 @@
             (((1,), (1,)), ((), ())),
             preferred_element_type=jnp.float32,
         )
-    split(s.reshape(2, 2, RA // 2, TT), xh == xl, core, keep, send)
-
-
-def score(pos, pieces, train, chunk, first, steps):
+    split(s.reshape(2, 2, RA // 2, -1), xh == xl, core, keep, send)
+
+
+def score(pos, pieces, train, chunk, first, steps, TT=TT):
     return pl.pallas_call(
         functools.partial(score_kernel, chunk),
         grid=(steps,),
@@ -263,7 +264,8 @@
         back = lax.ppermute(away, "layers", XL)
         total = keep[0] + got[0].astype(jnp.float32) + back.astype(jnp.float32)
         width = total.shape[1]
-        return lax.dynamic_update_slice(out, total.reshape(8, 1, SUB, width), (0, chunk, 0, first * TT)), away, back
+        out = lax.dynamic_update_slice(out, total.reshape(8, 1, SUB, width), (0, chunk, 0, first * TT))
+        return with_layout_constraint(out, Layout((0, 1, 2, 3))), away, back
 
     keep, send = part(pos, pieces, train, last_blocks(0), acc, True)
     send, pieces[14] = lax.optimization_barrier((send, pieces[14]))
@@ -273,7 +275,7 @@
     send, _ = lax.optimization_barrier((send, back))
     out, away, _ = reduce(out, keep, send, 1, 0)
     pos2, _ = lax.optimization_barrier((pos1, away))
-    out, _, _ = reduce(out, *score(pos2, pieces, train, 1, 3, 1), 1, 3)
+    out, _, _ = reduce(out, *score(pos2, pieces, train, 1, 6, 2, TT // 2), 1, 3)
     return out.reshape(256, NTL)
 
 

time: 151 us -> 150 us (level)
    dynamic_update_slice x4 -> x3, local copies, waits for them, and re-layouts: 1.82 us -> 0.28 us  [reduce(): lax.dynamic_update_slice(out, total.reshape(8, 1, SUB, width), (0, chunk,...]
    unnamed x8 -> x10, local copies, waits for them, and re-layouts: 2.79 us -> 4.1 us
where the time goes in v3:
time: 150 us
  starting transfers between devices  49.2 us (33%)
  waiting for transfers between devices  48.9 us (33%)
  Pallas kernels  42.9 us (29%)
  local copies, waits for them, and re-layouts  7.64 us (5%)
    ppermute x24, waiting for transfers between devices, send4(): lax.ppermute(x, 'rows', perm)  34.7 us
    ppermute x24, starting transfers between devices, send4(): lax.ppermute(x, 'rows', perm)  27.8 us
    pallas_call x3, Pallas kernels, part(): pl.pallas_call(functools.partial(part_kernel, blocks, acc is None, final)...  21.8 us
    pallas_call x2, Pallas kernels, score(): pl.pallas_call(functools.partial(score_kernel, chunk), grid=(steps,), out...  16.9 us
    ppermute x3, starting transfers between devices, reduce(): got = lax.ppermute(send, 'layers', CORE)  8.87 us
    ppermute x3, waiting for transfers between devices, reduce(): back = lax.ppermute(away, 'layers', XL)  5.1 us
    ppermute x3, waiting for transfers between devices, reduce(): got = lax.ppermute(send, 'layers', CORE)  4.97 us
    pallas_call x1, Pallas kernels, condition(): pl.pallas_call(condition_kernel, out_shape=jax.ShapeDtypeStruct((2, 2, RA...  4.17 us
  transfers between devices with their start and end apart: 36, of which 19 were waited for; matrix products, arithmetic and copies ran while one was open for 3% of the time, Pallas kernels for 26%

profile of v3, /device:TPU:1, one launch (start us, length us, event | category | flops | bytes accessed | tf_op | source)
XLA Modules:
  0.0 150.0 jit_solution(13751902035174634749)
XLA Ops:
  0.0 2.5 %collective-permute-start.2 = (bf16[2,16,4096]{2,1,0:T(8,128)(2,1)}, bf16[2,16,4096]{2,1,0:T(8,128)(2,1)S(1)}, u32[]{:S(2)}, u32[]{:S(2)}) collective-permute-start(bf16[2,16,4096]{2,1,0:T(8,128)(2,1)} %bitcast.37), channel_id=1, source_target_pairs={{0,16},{4,20},{8,24},{12,28},{16,32},{20,36},{24,40},{28,44},{32,4... | collective-permute-start | bytes 786440 | tf_op jit(solution)/shard_map/ppermute | solution.py:41
  2.5 2.7 %collective-permute-start.1 = (bf16[2,16,4096]{2,1,0:T(8,128)(2,1)}, bf16[2,16,4096]{2,1,0:T(8,128)(2,1)S(1)}, u32[]{:S(2)}, u32[]{:S(2)}) collective-permute-start(bf16[2,16,4096]{2,1,0:T(8,128)(2,1)} %bitcast.38), channel_id=1, source_target_pairs={{0,12},{4,0},{8,4},{12,8},{16,28},{20,16},{24,20},{28,24},{32,44},... | collective-permute-start | bytes 786440 | tf_op jit(solution)/shard_map/ppermute | solution.py:41
  5.2 2.1 %collective-permute-start.3 = (bf16[2,16,4096]{2,1,0:T(8,128)(2,1)}, bf16[2,16,4096]{2,1,0:T(8,128)(2,1)S(1)}, u32[]{:S(2)}, u32[]{:S(2)}) collective-permute-start(bf16[2,16,4096]{2,1,0:T(8,128)(2,1)} %bitcast.39), channel_id=1, source_target_pairs={{0,48},{4,52},{8,56},{12,60},{16,0},{20,4},{24,8},{28,12},{32,16},... | collective-permute-start | bytes 786440 | tf_op jit(solution)/shard_map/ppermute | solution.py:41
  7.3 2.7 %collective-permute-start.14 = (bf16[4096,128]{1,0:T(8,128)(2,1)}, bf16[4096,128]{1,0:T(8,128)(2,1)}, u32[]{:S(2)}, u32[]{:S(2)}) collective-permute-start(bf16[4096,128]{1,0:T(8,128)(2,1)} %bitcast.34), channel_id=1, source_target_pairs={{0,64},{4,68},{8,72},{12,76},{16,80},{20,84},{24,88},{28,92},{32,9... | collective-permute-start | bytes 3145736 | tf_op jit(solution)/shard_map/ppermute | solution.py:252
  12.4 2.9 %collective-permute-start.5 = (bf16[3,16,4096]{2,1,0:T(8,128)(2,1)S(1)}, bf16[3,16,4096]{2,1,0:T(8,128)(2,1)S(1)}, u32[]{:S(2)}, u32[]{:S(2)}) collective-permute-start(bf16[3,16,4096]{2,1,0:T(8,128)(2,1)S(1)} %pad_maximum_fusion.6), channel_id=1, source_target_pairs={{0,12},{4,0},{8,4},{12,8},{16,28},{20,16},{24,20},{28,24},{32,44},... | collective-permute-start | bytes 1179656 | tf_op jit(solution)/shard_map/ppermute | solution.py:41
  17.6 4.1 %collective-permute-done.6.refs_7_ = bf16[3,16,4096]{2,1,0:T(8,128)(2,1)S(1)} collective-permute-done((bf16[3,16,4096]{2,1,0:T(8,128)(2,1)S(1)}, bf16[3,16,4096]{2,1,0:T(8,128)(2,1)S(1)}, u32[]{:S(2)}, u32[]{:S(2)}) %collective-permute-start.6) | collective-permute-done | bytes 393248 | tf_op jit(solution)/shard_map/ppermute | solution.py:41
  21.7 3.0 %collective-permute-start.12 = (bf16[16,4096]{1,0:T(8,128)(2,1)S(1)}, bf16[16,4096]{1,0:T(8,128)(2,1)S(1)}, u32[]{:S(2)}, u32[]{:S(2)}) collective-permute-start(bf16[16,4096]{1,0:T(8,128)(2,1)S(1)} %slice_bitcast_fusion.3), channel_id=1, source_target_pairs={{0,8},{4,12},{8,0},{12,4},{16,24},{20,28},{24,16},{28,20},{32,40},... | collective-permute-start | bytes 393224 | tf_op jit(solution)/shard_map/ppermute | solution.py:57
  30.4 2.7 %collective-permute-start.11 = (bf16[2,16,4096]{2,1,0:T(8,128)(2,1)}, bf16[2,16,4096]{2,1,0:T(8,128)(2,1)}, u32[]{:S(2)}, u32[]{:S(2)}) collective-permute-start(bf16[2,16,4096]{2,1,0:T(8,128)(2,1)} %slice.135), channel_id=1, source_target_pairs={{0,48},{4,52},{8,56},{12,60},{16,0},{20,4},{24,8},{28,12},{32,16},... | collective-permute-start | bytes 786440 | tf_op jit(solution)/shard_map/ppermute | solution.py:41
  36.7 3.8 %collective-permute-done.8.refs_9_ = bf16[2,16,4096]{2,1,0:T(8,128)(2,1)} collective-permute-done((bf16[2,16,4096]{2,1,0:T(8,128)(2,1)}, bf16[2,16,4096]{2,1,0:T(8,128)(2,1)}, u32[]{:S(2)}, u32[]{:S(2)}) %collective-permute-start.8) | collective-permute-done | bytes 262176 | tf_op jit(solution)/shard_map/ppermute | solution.py:41
  42.6 4.2 %condition.1 = bf16[2,2,256,128]{3,2,1,0:T(8,128)(2,1)S(1)} custom-call(s32[5]{0:T(128)S(1)} %stack.32.pos, bf16[2,16,4096]{2,1,0:T(8,128)(2,1)S(1)} %bitcast.41, bf16[2,16,4096]{2,1,0:T(8,128)(2,1)S(1)} %collective-permute-done.refs_1_, bf16[2,16,4096]{2,1,0:T(8,128)(2,1)S(1)} %collective-permute-done.1.refs_2_, ...), custom_call_target="tpu_custom_call" | custom-call | flops 1073741824 | bytes 6291456 | tf_op jit(solution)/shard_map/condition/pallas_call | solution.py:88
  46.8 2.7 %collective-permute-start.15 = (bf16[2,2,256,128]{3,2,1,0:T(8,128)(2,1)S(1)}, bf16[2,2,256,128]{3,2,1,0:T(8,128)(2,1)S(1)}, u32[]{:S(2)}, u32[]{:S(2)}) collective-permute-start(bf16[2,2,256,128]{3,2,1,0:T(8,128)(2,1)S(1)} %condition.1), channel_id=1, source_target_pairs={{0,64},{4,68},{8,72},{12,76},{16,80},{20,84},{24,88},{28,92},{32,9... | collective-permute-start | bytes 786440 | tf_op jit(solution)/shard_map/ppermute | solution.py:255
  49.5 4.1 %collective-permute-done.15 = bf16[2,2,256,128]{3,2,1,0:T(8,128)(2,1)S(1)} collective-permute-done((bf16[2,2,256,128]{3,2,1,0:T(8,128)(2,1)S(1)}, bf16[2,2,256,128]{3,2,1,0:T(8,128)(2,1)S(1)}, u32[]{:S(2)}, u32[]{:S(2)}) %collective-permute-start.15) | collective-permute-done | bytes 262176 | tf_op jit(solution)/shard_map/ppermute | solution.py:255
  53.9 2.6 %collective-permute-start.20 = (bf16[2,2,2,256,128]{4,3,2,1,0:T(8,128)(2,1)S(1)}, bf16[2,2,2,256,128]{4,3,2,1,0:T(8,128)(2,1)S(1)}, u32[]{:S(2)}, u32[]{:S(2)}) collective-permute-start(bf16[2,2,2,256,128]{4,3,2,1,0:T(8,128)(2,1)S(1)} %pad_maximum_fusion.4.refs_0_), channel_id=1, source_target_pairs={{0,48},{4,52},{8,56},{12,60},{16,0},{20,4},{24,8},{28,12},{32,16},... | collective-permute-start | bytes 1572872 | tf_op jit(solution)/shard_map/ppermute | solution.py:41
  57.9 5.1 %collective-permute-done.16.refs_3_ = bf16[2,2,2,256,128]{4,3,2,1,0:T(8,128)(2,1)S(1)} collective-permute-done((bf16[2,2,2,256,128]{4,3,2,1,0:T(8,128)(2,1)S(1)}, bf16[2,2,2,256,128]{4,3,2,1,0:T(8,128)(2,1)S(1)}, u32[]{:S(2)}, u32[]{:S(2)}) %collective-permute-start.16) | collective-permute-done | bytes 524320 | tf_op jit(solution)/shard_map/ppermute | solution.py:41
  63.2 2.7 %collective-permute-done.17.refs_1_ = bf16[2,2,2,256,128]{4,3,2,1,0:T(8,128)(2,1)S(1)} collective-permute-done((bf16[2,2,2,256,128]{4,3,2,1,0:T(8,128)(2,1)S(1)}, bf16[2,2,2,256,128]{4,3,2,1,0:T(8,128)(2,1)S(1)}, u32[]{:S(2)}, u32[]{:S(2)}) %collective-permute-start.17) | collective-permute-done | bytes 524320 | tf_op jit(solution)/shard_map/ppermute | solution.py:41
  67.9 11.1 %collective-permute-done.24.refs_2_.refs_7_ = bf16[3,2,2,256,128]{4,3,2,1,0:T(8,128)(2,1)S(1)} collective-permute-done((bf16[3,2,2,256,128]{4,3,2,1,0:T(8,128)(2,1)S(1)}, bf16[3,2,2,256,128]{4,3,2,1,0:T(8,128)(2,1)S(1)}, u32[]{:S(2)}, u32[]{:S(2)}) %collective-permute-start.24) | collective-permute-done | bytes 786464 | tf_op jit(solution)/shard_map/ppermute | solution.py:41
  79.3 6.9 %part.3.refs_16_ = f32[512,2048]{1,0:T(8,128)S(1)} custom-call(s32[5]{0:T(128)S(1)} %stack.32.pos, bf16[2,2,2,256,128]{4,3,2,1,0:T(8,128)(2,1)S(1)} %pad_maximum_fusion.4.refs_0_, bf16[2,2,2,256,128]{4,3,2,1,0:T(8,128)(2,1)S(1)} %collective-permute-done.17.refs_1_, bf16[2,2,2,256,128]{4,3,2,1,0:T(8,128)(2,1)S(1)} %collective-permute-done.21.refs_2_, ...), custom_call_target="tpu_custom_call" | custom-call | flops 2684354560 | bytes 13631488 | tf_op jit(solution)/shard_map/part/pallas_call | solution.py:175
  90.3 7.8 %part.4.refs_15_ = f32[512,2048]{1,0:T(8,128)S(1)} custom-call(s32[5]{0:T(128)S(1)} %stack.32.pos, bf16[3,2,2,256,128]{4,3,2,1,0:T(8,128)(2,1)S(1)} %collective-permute-done.18.refs_0_.refs_5_, bf16[3,2,2,256,128]{4,3,2,1,0:T(8,128)(2,1)S(1)} %collective-permute-done.22.refs_1_.refs_6_, ...), custom_call_target="tpu_custom_call" | custom-call | flops 3221225472 | bytes 14680064 | tf_op jit(solution)/shard_map/part/pallas_call | solution.py:175
  101.9 7.1 %part.5 = (f32[2,128,2048]{2,1,0:T(8,128)S(1)}, bf16[2,128,2048]{2,1,0:T(8,128)(2,1)S(1)}) custom-call(s32[5]{0:T(128)S(1)} %stack.32.pos, bf16[2,2,2,256,128]{4,3,2,1,0:T(8,128)(2,1)S(1)} %collective-permute-done.19.refs_0_.refs_9_, bf16[2,2,2,256,128]{4,3,2,1,0:T(8,128)(2,1)S(1)} %collective-permute-done.23.refs_1_.refs_10_, ...), custom_call_target="tpu_custom_call" | custom-call | flops 2684354560 | bytes 13631488 | tf_op jit(solution)/shard_map/part/pallas_call | solution.py:175
  109.0 6.9 %collective-permute-start.30 = (bf16[2,128,2048]{2,1,0:T(8,128)(2,1)S(1)}, bf16[2,128,2048]{2,1,0:T(8,128)(2,1)S(1)}, u32[]{:S(2)}, u32[]{:S(2)}) collective-permute-start(bf16[2,128,2048]{2,1,0:T(8,128)(2,1)S(1)} %get-tuple-element.18), channel_id=1, source_target_pairs={{0,1},{1,0},{2,3},{3,2},{4,5},{5,4},{6,7},{7,6},{8,9},{9,8},{10,11... | collective-permute-start | bytes 3145736 | tf_op jit(solution)/shard_map/ppermute | solution.py:262
  116.0 2.3 %collective-permute-done.30 = bf16[2,128,2048]{2,1,0:T(8,128)(2,1)S(1)} collective-permute-done((bf16[2,128,2048]{2,1,0:T(8,128)(2,1)S(1)}, bf16[2,128,2048]{2,1,0:T(8,128)(2,1)S(1)}, u32[]{:S(2)}, u32[]{:S(2)}) %collective-permute-start.30) | collective-permute-done | bytes 1048608 | tf_op jit(solution)/shard_map/ppermute | solution.py:262
  119.7 11.1 %score.2 = (f32[2,128,1536]{2,1,0:T(8,128)S(1)}, bf16[2,128,1536]{2,1,0:T(8,128)(2,1)S(1)}) custom-call(s32[5]{0:T(128)S(1)} %stack.32.pos, bf16[2,2,2,256,128]{4,3,2,1,0:T(8,128)(2,1)S(1)} %pad_maximum_fusion.4.refs_0_, bf16[2,2,2,256,128]{4,3,2,1,0:T(8,128)(2,1)S(1)} %collective-permute-done.17.refs_1_, ...), custom_call_target="tpu_custom_call" | custom-call | flops 6442450944 | bytes 16777216 | tf_op jit(solution)/shard_map/score/pallas_call | solution.py:223
  136.1 5.8 %score.3 = (f32[2,128,512]{2,1,0:T(8,128)S(1)}, bf16[2,128,512]{2,1,0:T(8,128)(2,1)S(1)}) custom-call(s32[5]{0:T(128)S(1)} %stack.32.pos, bf16[2,2,2,256,128]{4,3,2,1,0:T(8,128)(2,1)S(1)} %pad_maximum_fusion.4.refs_0_, bf16[2,2,2,256,128]{4,3,2,1,0:T(8,128)(2,1)S(1)} %collective-permute-done.17.refs_1_, ...), custom_call_target="tpu_custom_call" | custom-call | flops 2147483648 | bytes 8388608 | tf_op jit(solution)/shard_map/score/pallas_call | solution.py:223
  145.4 3.2 %collective-permute-done.35 = bf16[128,512]{1,0:T(8,128)(2,1)S(1)} collective-permute-done((bf16[128,512]{1,0:T(8,128)(2,1)S(1)}, bf16[128,512]{1,0:T(8,128)(2,1)S(1)}, u32[]{:S(2)}, u32[]{:S(2)}) %collective-permute-start.35) | collective-permute-done | bytes 131104 | tf_op jit(solution)/shard_map/ppermute | solution.py:264
  (103 shorter events, 39.5 us)
Async XLA Ops:
  0.0 10.8 %collective-permute-start.2 = (bf16[2,16,4096]{2,1,0:T(8,128)(2,1)}, bf16[2,16,4096]{2,1,0:T(8,128)(2,1)S(1)}, u32[]{:S(2)}, u32[]{:S(2)}) collective-permute-start(bf16[2,16,4096]{2,1,0:T(8,128)(2,1)} %bitcast.37), channel_id=1, source_target_pairs={{0,16},{4,20},{8,24},{12,28},{16,32},{20,36},{24,40},{28,44},{32,4... | collective-permute-start | bytes 786440 | tf_op jit(solution)/shard_map/ppermute | solution.py:41
  7.3 33.2 %collective-permute-start.14 = (bf16[4096,128]{1,0:T(8,128)(2,1)}, bf16[4096,128]{1,0:T(8,128)(2,1)}, u32[]{:S(2)}, u32[]{:S(2)}) collective-permute-start(bf16[4096,128]{1,0:T(8,128)(2,1)} %bitcast.34), channel_id=1, source_target_pairs={{0,64},{4,68},{8,72},{12,76},{16,80},{20,84},{24,88},{28,92},{32,9... | collective-permute-start | bytes 3145736 | tf_op jit(solution)/shard_map/ppermute | solution.py:252
  10.9 10.8 %collective-permute-start.6 = (bf16[3,16,4096]{2,1,0:T(8,128)(2,1)S(1)}, bf16[3,16,4096]{2,1,0:T(8,128)(2,1)S(1)}, u32[]{:S(2)}, u32[]{:S(2)}) collective-permute-start(bf16[3,16,4096]{2,1,0:T(8,128)(2,1)S(1)} %pad_maximum_fusion.7), channel_id=1, source_target_pairs={{0,16},{4,20},{8,24},{12,28},{16,32},{20,36},{24,40},{28,44},{32,4... | collective-permute-start | bytes 1179656 | tf_op jit(solution)/shard_map/ppermute | solution.py:41
  12.4 12.2 %collective-permute-start.5 = (bf16[3,16,4096]{2,1,0:T(8,128)(2,1)S(1)}, bf16[3,16,4096]{2,1,0:T(8,128)(2,1)S(1)}, u32[]{:S(2)}, u32[]{:S(2)}) collective-permute-start(bf16[3,16,4096]{2,1,0:T(8,128)(2,1)S(1)} %pad_maximum_fusion.6), channel_id=1, source_target_pairs={{0,12},{4,0},{8,4},{12,8},{16,28},{20,16},{24,20},{28,24},{32,44},... | collective-permute-start | bytes 1179656 | tf_op jit(solution)/shard_map/ppermute | solution.py:41
  15.5 10.9 %collective-permute-start.7 = (bf16[3,16,4096]{2,1,0:T(8,128)(2,1)S(1)}, bf16[3,16,4096]{2,1,0:T(8,128)(2,1)S(1)}, u32[]{:S(2)}, u32[]{:S(2)}) collective-permute-start(bf16[3,16,4096]{2,1,0:T(8,128)(2,1)S(1)} %pad_maximum_fusion.8), channel_id=1, source_target_pairs={{0,48},{4,52},{8,56},{12,60},{16,0},{20,4},{24,8},{28,12},{32,16},... | collective-permute-start | bytes 1179656 | tf_op jit(solution)/shard_map/ppermute | solution.py:41
  16.8 10.8 %collective-permute-start.4 = (bf16[3,16,4096]{2,1,0:T(8,128)(2,1)S(1)}, bf16[3,16,4096]{2,1,0:T(8,128)(2,1)S(1)}, u32[]{:S(2)}, u32[]{:S(2)}) collective-permute-start(bf16[3,16,4096]{2,1,0:T(8,128)(2,1)S(1)} %pad_maximum_fusion.5), channel_id=1, source_target_pairs={{0,4},{4,8},{8,12},{12,0},{16,20},{20,24},{24,28},{28,16},{32,36},... | collective-permute-start | bytes 1179656 | tf_op jit(solution)/shard_map/ppermute | solution.py:41
  21.7 8.7 %collective-permute-start.12 = (bf16[16,4096]{1,0:T(8,128)(2,1)S(1)}, bf16[16,4096]{1,0:T(8,128)(2,1)S(1)}, u32[]{:S(2)}, u32[]{:S(2)}) collective-permute-start(bf16[16,4096]{1,0:T(8,128)(2,1)S(1)} %slice_bitcast_fusion.3), channel_id=1, source_target_pairs={{0,8},{4,12},{8,0},{12,4},{16,24},{20,28},{24,16},{28,20},{32,40},... | collective-permute-start | bytes 393224 | tf_op jit(solution)/shard_map/ppermute | solution.py:57
  53.7 9.3 %collective-permute-start.16 = (bf16[2,2,2,256,128]{4,3,2,1,0:T(8,128)(2,1)S(1)}, bf16[2,2,2,256,128]{4,3,2,1,0:T(8,128)(2,1)S(1)}, u32[]{:S(2)}, u32[]{:S(2)}) collective-permute-start(bf16[2,2,2,256,128]{4,3,2,1,0:T(8,128)(2,1)S(1)} %pad_maximum_fusion.4.refs_0_), channel_id=1, source_target_pairs={{0,16},{4,20},{8,24},{12,28},{16,32},{20,36},{24,40},{28,44},{32,4... | collective-permute-start | bytes 1572872 | tf_op jit(solution)/shard_map/ppermute | solution.py:41
  53.8 9.3 %collective-permute-start.21 = (bf16[2,2,2,256,128]{4,3,2,1,0:T(8,128)(2,1)S(1)}, bf16[2,2,2,256,128]{4,3,2,1,0:T(8,128)(2,1)S(1)}, u32[]{:S(2)}, u32[]{:S(2)}) collective-permute-start(bf16[2,2,2,256,128]{4,3,2,1,0:T(8,128)(2,1)S(1)} %pad_maximum_fusion.4.refs_0_), channel_id=1, source_target_pairs={{0,12},{4,0},{8,4},{12,8},{16,28},{20,16},{24,20},{28,24},{32,44},... | collective-permute-start | bytes 1572872 | tf_op jit(solution)/shard_map/ppermute | solution.py:41
  53.9 9.3 %collective-permute-start.20 = (bf16[2,2,2,256,128]{4,3,2,1,0:T(8,128)(2,1)S(1)}, bf16[2,2,2,256,128]{4,3,2,1,0:T(8,128)(2,1)S(1)}, u32[]{:S(2)}, u32[]{:S(2)}) collective-permute-start(bf16[2,2,2,256,128]{4,3,2,1,0:T(8,128)(2,1)S(1)} %pad_maximum_fusion.4.refs_0_), channel_id=1, source_target_pairs={{0,48},{4,52},{8,56},{12,60},{16,0},{20,4},{24,8},{28,12},{32,16},... | collective-permute-start | bytes 1572872 | tf_op jit(solution)/shard_map/ppermute | solution.py:41
  56.4 9.5 %collective-permute-start.17 = (bf16[2,2,2,256,128]{4,3,2,1,0:T(8,128)(2,1)S(1)}, bf16[2,2,2,256,128]{4,3,2,1,0:T(8,128)(2,1)S(1)}, u32[]{:S(2)}, u32[]{:S(2)}) collective-permute-start(bf16[2,2,2,256,128]{4,3,2,1,0:T(8,128)(2,1)S(1)} %pad_maximum_fusion.4.refs_0_), channel_id=1, source_target_pairs={{0,4},{4,8},{8,12},{12,0},{16,20},{20,24},{24,28},{28,16},{32,36},... | collective-permute-start | bytes 1572872 | tf_op jit(solution)/shard_map/ppermute | solution.py:41
  63.1 15.9 %collective-permute-start.24 = (bf16[3,2,2,256,128]{4,3,2,1,0:T(8,128)(2,1)S(1)}, bf16[3,2,2,256,128]{4,3,2,1,0:T(8,128)(2,1)S(1)}, u32[]{:S(2)}, u32[]{:S(2)}) collective-permute-start(bf16[3,2,2,256,128]{4,3,2,1,0:T(8,128)(2,1)S(1)} %pad_maximum_fusion.2), channel_id=1, source_target_pairs={{0,16},{4,20},{8,24},{12,28},{16,32},{20,36},{24,40},{28,44},{32,4... | collective-permute-start | bytes 2359304 | tf_op jit(solution)/shard_map/ppermute | solution.py:41
  66.0 20.1 %collective-permute-start.26 = (bf16[3,2,2,256,128]{4,3,2,1,0:T(8,128)(2,1)S(1)}, bf16[3,2,2,256,128]{4,3,2,1,0:T(8,128)(2,1)S(1)}, u32[]{:S(2)}, u32[]{:S(2)}) collective-permute-start(bf16[3,2,2,256,128]{4,3,2,1,0:T(8,128)(2,1)S(1)} %pad_maximum_fusion.3), channel_id=1, source_target_pairs={{0,48},{4,52},{8,56},{12,60},{16,0},{20,4},{24,8},{28,12},{32,16},... | collective-permute-start | bytes 2359304 | tf_op jit(solution)/shard_map/ppermute | solution.py:41
  66.2 21.6 %collective-permute-start.22 = (bf16[3,2,2,256,128]{4,3,2,1,0:T(8,128)(2,1)S(1)}, bf16[3,2,2,256,128]{4,3,2,1,0:T(8,128)(2,1)S(1)}, u32[]{:S(2)}, u32[]{:S(2)}) collective-permute-start(bf16[3,2,2,256,128]{4,3,2,1,0:T(8,128)(2,1)S(1)} %pad_maximum_fusion.1), channel_id=1, source_target_pairs={{0,12},{4,0},{8,4},{12,8},{16,28},{20,16},{24,20},{28,24},{32,44},... | collective-permute-start | bytes 2359304 | tf_op jit(solution)/shard_map/ppermute | solution.py:41
  66.4 23.0 %collective-permute-start.18 = (bf16[3,2,2,256,128]{4,3,2,1,0:T(8,128)(2,1)S(1)}, bf16[3,2,2,256,128]{4,3,2,1,0:T(8,128)(2,1)S(1)}, u32[]{:S(2)}, u32[]{:S(2)}) collective-permute-start(bf16[3,2,2,256,128]{4,3,2,1,0:T(8,128)(2,1)S(1)} %pad_maximum_fusion), channel_id=1, source_target_pairs={{0,4},{4,8},{8,12},{12,0},{16,20},{20,24},{24,28},{28,16},{32,36},... | collective-permute-start | bytes 2359304 | tf_op jit(solution)/shard_map/ppermute | solution.py:41
  79.0 10.6 %collective-permute-start.28 = (bf16[2,2,256,128]{3,2,1,0:T(8,128)(2,1)S(1)}, bf16[2,2,256,128]{3,2,1,0:T(8,128)(2,1)S(1)}, u32[]{:S(2)}, u32[]{:S(2)}) collective-permute-start(bf16[2,2,256,128]{3,2,1,0:T(8,128)(2,1)S(1)} %slice_bitcast_fusion.1), channel_id=1, source_target_pairs={{0,8},{4,12},{8,0},{12,4},{16,24},{20,28},{24,16},{28,20},{32,40},... | collective-permute-start | bytes 786440 | tf_op jit(solution)/shard_map/ppermute | solution.py:57
  86.2 11.8 %collective-permute-start.27 = (bf16[2,2,2,256,128]{4,3,2,1,0:T(8,128)(2,1)S(1)}, bf16[2,2,2,256,128]{4,3,2,1,0:T(8,128)(2,1)S(1)}, u32[]{:S(2)}, u32[]{:S(2)}) collective-permute-start(bf16[2,2,2,256,128]{4,3,2,1,0:T(8,128)(2,1)S(1)} %slice.145), channel_id=1, source_target_pairs={{0,48},{4,52},{8,56},{12,60},{16,0},{20,4},{24,8},{28,12},{32,16},... | collective-permute-start | bytes 1572872 | tf_op jit(solution)/shard_map/ppermute | solution.py:41
  87.2 12.4 %collective-permute-start.25 = (bf16[2,2,2,256,128]{4,3,2,1,0:T(8,128)(2,1)S(1)}, bf16[2,2,2,256,128]{4,3,2,1,0:T(8,128)(2,1)S(1)}, u32[]{:S(2)}, u32[]{:S(2)}) collective-permute-start(bf16[2,2,2,256,128]{4,3,2,1,0:T(8,128)(2,1)S(1)} %slice.143), channel_id=1, source_target_pairs={{0,16},{4,20},{8,24},{12,28},{16,32},{20,36},{24,40},{28,44},{32,4... | collective-permute-start | bytes 1572872 | tf_op jit(solution)/shard_map/ppermute | solution.py:41
  87.9 12.3 %collective-permute-start.23 = (bf16[2,2,2,256,128]{4,3,2,1,0:T(8,128)(2,1)S(1)}, bf16[2,2,2,256,128]{4,3,2,1,0:T(8,128)(2,1)S(1)}, u32[]{:S(2)}, u32[]{:S(2)}) collective-permute-start(bf16[2,2,2,256,128]{4,3,2,1,0:T(8,128)(2,1)S(1)} %slice.141), channel_id=1, source_target_pairs={{0,12},{4,0},{8,4},{12,8},{16,28},{20,16},{24,20},{28,24},{32,44},... | collective-permute-start | bytes 1572872 | tf_op jit(solution)/shard_map/ppermute | solution.py:41
  89.5 12.4 %collective-permute-start.19 = (bf16[2,2,2,256,128]{4,3,2,1,0:T(8,128)(2,1)S(1)}, bf16[2,2,2,256,128]{4,3,2,1,0:T(8,128)(2,1)S(1)}, u32[]{:S(2)}, u32[]{:S(2)}) collective-permute-start(bf16[2,2,2,256,128]{4,3,2,1,0:T(8,128)(2,1)S(1)} %slice.139), channel_id=1, source_target_pairs={{0,4},{4,8},{8,12},{12,0},{16,20},{20,24},{24,28},{28,16},{32,36},... | collective-permute-start | bytes 1572872 | tf_op jit(solution)/shard_map/ppermute | solution.py:41
  89.6 19.4 %collective-permute-start.29 = (bf16[2,2,256,128]{3,2,1,0:T(8,128)(2,1)S(1)}, bf16[2,2,256,128]{3,2,1,0:T(8,128)(2,1)S(1)}, u32[]{:S(2)}, u32[]{:S(2)}) collective-permute-start(bf16[2,2,256,128]{3,2,1,0:T(8,128)(2,1)S(1)} %slice_bitcast_fusion), channel_id=1, source_target_pairs={{0,32},{4,36},{8,40},{12,44},{16,48},{20,52},{24,56},{28,60},{32,0... | collective-permute-start | bytes 786440 | tf_op jit(solution)/shard_map/ppermute | solution.py:59
  109.0 9.2 %collective-permute-start.30 = (bf16[2,128,2048]{2,1,0:T(8,128)(2,1)S(1)}, bf16[2,128,2048]{2,1,0:T(8,128)(2,1)S(1)}, u32[]{:S(2)}, u32[]{:S(2)}) collective-permute-start(bf16[2,128,2048]{2,1,0:T(8,128)(2,1)S(1)} %get-tuple-element.18), channel_id=1, source_target_pairs={{0,1},{1,0},{2,3},{3,2},{4,5},{5,4},{6,7},{7,6},{8,9},{9,8},{10,11... | collective-permute-start | bytes 3145736 | tf_op jit(solution)/shard_map/ppermute | solution.py:262
  118.4 13.2 %collective-permute-start.31 = (bf16[128,2048]{1,0:T(8,128)(2,1)S(1)}, bf16[128,2048]{1,0:T(8,128)(2,1)S(1)}, u32[]{:S(2)}, u32[]{:S(2)}) collective-permute-start(bf16[128,2048]{1,0:T(8,128)(2,1)S(1)} %fusion), channel_id=1, source_target_pairs={{0,2},{2,0},{1,3},{3,1},{4,6},{6,4},{5,7},{7,5},{8,10},{10,8},{9,1... | collective-permute-start | bytes 1572872 | tf_op jit(solution)/shard_map/ppermute | solution.py:264
  134.8 10.4 %collective-permute-start.33 = (bf16[128,1536]{1,0:T(8,128)(2,1)S(1)}, bf16[128,1536]{1,0:T(8,128)(2,1)S(1)}, u32[]{:S(2)}, u32[]{:S(2)}) collective-permute-start(bf16[128,1536]{1,0:T(8,128)(2,1)S(1)} %fusion.1), channel_id=1, source_target_pairs={{0,2},{2,0},{1,3},{3,1},{4,6},{6,4},{5,7},{7,5},{8,10},{10,8},{9,1... | collective-permute-start | bytes 1179656 | tf_op jit(solution)/shard_map/ppermute | solution.py:264
  (17 other events, 106.8 us)
